TPU v7x, 32 devices: a whole 2x2x4 slice. The times are simulated.
32 devices in a mesh: dp: 4 (over y, x), seq: 2 (over core), head: 4 (over z).
Axes of the slice: x: 2, y: 2, z: 4, core: 2. Of those that a mesh axis runs over, the one named last changes fastest.
Arguments:
- tokens: bfloat16 [4, 1024, 2048], P('dp', 'seq'), may hold values from -6 to 6
- attn_gain: float32 [2048], replicated, may hold values from 0.1 to 1.9
- w_qkvg: bfloat16 [4, 2048, 2048], P(None, None, 'head'), may hold values from -0.125 to 0.125
- w_beta: bfloat16 [2048, 16], P(None, 'head'), may hold values from -0.25 to 0.25
- conv_w: float32 [3, 4, 2048], P(None, None, 'head'), may hold values from -3 to 3
- out_gain: float32 [128], replicated, may hold values from 0.1 to 1.9
- w_o: bfloat16 [2048, 2048], P('head'), may hold values from -0.125 to 0.125
- mlp_gain: float32 [2048], replicated, may hold values from 0.1 to 1.9
- w_gateup: bfloat16 [2, 2048, 5632], P(None, None, 'head'), may hold values from -0.125 to 0.125
- w_down: bfloat16 [5632, 2048], P('head'), may hold values from -0.078125 to 0.078125
- cotangent: bfloat16 [4, 1024, 2048], P('dp', 'seq'), may hold values from -6 to 6
Outputs:
- out: bfloat16 [4, 1024, 2048], P('dp', 'seq')
- grad_tokens: bfloat16 [4, 1024, 2048], P('dp', 'seq')
- grad_attn_gain: float32 [2048], replicated
- grad_w_qkvg: float32 [4, 2048, 2048], P(None, ('dp', 'seq'), 'head')
- grad_w_beta: float32 [2048, 16], P(None, 'head')
- grad_conv_w: float32 [3, 4, 2048], P(None, None, 'head')
- grad_out_gain: float32 [128], replicated
- grad_w_o: float32 [2048, 2048], P('head', ('dp', 'seq'))
- grad_mlp_gain: float32 [2048], replicated
- grad_w_gateup: float32 [2, 2048, 5632], P(None, ('dp', 'seq'), 'head')
- grad_w_down: float32 [5632, 2048], P('head', ('dp', 'seq'))
- state_mean: float32 [], replicated
All inputs are finite; a program needn't handle non-finite values.
Results may differ from a plain program's by a relative error of at most 0.012.
The roundings to bfloat16 on the way count: a program that leaves them out, or rounds other values in their place, can miss the bound.
Values may be sent and summed in bfloat16 or wider, within the bound.
A program may use at most 320 MiB of HBM per device.

v0:
```python
import jax
import jax.numpy as jnp
from jax import lax
from jax.sharding import PartitionSpec as P

H = 16
HD = 128
SPAN = 64


FULL_PRECISION = lax.Precision.HIGHEST


def from_behind(x, axis, by):
    size = lax.axis_size(axis)
    pairs = [(i, i + by) for i in range(size) if 0 <= i + by < size]
    return lax.ppermute(x, axis, pairs)


def rms_scale(values, gain_vec):
    return values * lax.rsqrt(jnp.mean(values * values, axis=-1, keepdims=True) + 1e-06) * gain_vec


def unit_rows(values):
    return values * lax.rsqrt(jnp.sum(values * values, axis=-1, keepdims=True) + 1e-06)


def to_blocks(values, head_count):
    count_rows = values.shape[0]
    return values.reshape(count_rows // SPAN, SPAN, head_count, HD).transpose(0, 2, 1, 3)


def prepare(raw_ext, conv_w, beta_logit):
    count_rows, head_count = beta_logit.shape
    taps_count = conv_w.shape[1]
    conv_sum = conv_w[:, 0] * raw_ext[0:count_rows]
    for tap_index in range(1, taps_count):
        conv_sum = conv_sum + conv_w[:, tap_index] * raw_ext[tap_index : tap_index + count_rows]
    active = jax.nn.silu(conv_sum)
    queries = unit_rows(active[:, 0].reshape(count_rows, head_count, HD)) * HD ** (-0.5)
    key_vectors = unit_rows(active[:, 1].reshape(count_rows, head_count, HD))
    value_rows = active[:, 2].reshape(count_rows, head_count, HD)
    beta_blocks = (
        jax.nn.sigmoid(beta_logit)
        .reshape(count_rows // SPAN, SPAN, head_count)
        .transpose(0, 2, 1)[..., None]
    )
    query_blocks = to_blocks(queries, head_count)
    key_blocks = to_blocks(key_vectors, head_count)
    scaled = key_blocks * beta_blocks
    gram_blocks = jnp.einsum("nhik,nhjk->nhij", scaled, key_blocks, precision=FULL_PRECISION)
    system = jnp.eye(SPAN, dtype=jnp.float32) + jnp.tril(gram_blocks, -1)
    householder_keys = jax.scipy.linalg.solve_triangular(
        system, scaled, lower=True, unit_diagonal=True
    )
    householder_values = jax.scipy.linalg.solve_triangular(
        system, to_blocks(value_rows, head_count) * beta_blocks, lower=True, unit_diagonal=True
    )
    return (query_blocks, key_blocks, householder_keys, householder_values)


def run_states(start_state, key_blocks, householder_keys, householder_values):

    def advance(running_state, pieces):
        key_vectors, weighted_keys, weighted_values = pieces
        update_rows = weighted_values - jnp.einsum(
            "nij,njq->niq", weighted_keys, running_state, precision=FULL_PRECISION
        )
        return (
            running_state
            + jnp.einsum("xea,xef->xaf", key_vectors, update_rows, precision=FULL_PRECISION),
            running_state,
        )

    return lax.scan(advance, start_state, (key_blocks, householder_keys, householder_values))


def finish(
    start_state, query_blocks, key_blocks, householder_keys, householder_values, gate_pre, out_gain
):
    end_state, before = run_states(start_state, key_blocks, householder_keys, householder_values)
    update_rows = householder_values - jnp.einsum(
        "nhck,nhkv->nhcv", householder_keys, before, precision=FULL_PRECISION
    )
    span_len = query_blocks.shape[2]
    causal = jnp.tril(jnp.ones((span_len, span_len), jnp.float32))
    attention_logits = (
        jnp.einsum("nhik,nhjk->nhij", query_blocks, key_blocks, precision=FULL_PRECISION) * causal
    )
    block_results = jnp.einsum(
        "nhck,nhkv->nhcv", query_blocks, before, precision=FULL_PRECISION
    ) + jnp.einsum("nhij,nhjv->nhiv", attention_logits, update_rows, precision=FULL_PRECISION)
    count_rows = gate_pre.shape[0]
    head_count = query_blocks.shape[1]
    outputs = block_results.transpose(0, 2, 1, 3).reshape(count_rows, head_count, HD)
    gate_heads = gate_pre.reshape(count_rows, head_count, HD)
    gated_rows = (
        outputs
        * lax.rsqrt(jnp.mean(outputs * outputs, axis=-1, keepdims=True) + 1e-05)
        * out_gain
        * jax.nn.silu(gate_heads)
    )
    return (gated_rows.reshape(count_rows, head_count * HD), end_state)


def apply_map(matrix, state_in, shift_term):
    return jnp.einsum("qkw,qwu->qku", matrix, state_in, precision=FULL_PRECISION) + shift_term


def per_device(
    tokens, attn_gain, w_qkvg, w_beta, conv_w, out_gain, w_o, mlp_gain, w_gateup, w_down, cotangent
):
    tok_rows = tokens[0].astype(jnp.float32)
    count_rows = tok_rows.shape[0]
    head_count = w_beta.shape[1]
    rim_width = conv_w.shape[1] - 1
    normed_low = rms_scale(tok_rows, attn_gain).astype(jnp.bfloat16)
    projected = jnp.einsum("td,cde->tce", normed_low, w_qkvg, preferred_element_type=jnp.float32)
    raw_low = projected[:, :3].astype(jnp.bfloat16)
    gate_pre = projected[:, 3]
    beta_logit = jnp.dot(normed_low, w_beta, preferred_element_type=jnp.float32)
    rim_rows = from_behind(raw_low[count_rows - rim_width :], "seq", 1)
    raw_ext = jnp.concatenate([rim_rows, raw_low], axis=0).astype(jnp.float32)
    prepared, prep_back = jax.vjp(prepare, raw_ext, conv_w, beta_logit)
    query_blocks, key_blocks, householder_keys, householder_values = prepared
    identity = jnp.broadcast_to(jnp.eye(HD, dtype=jnp.float32), (head_count, HD, HD))
    no_state = jnp.zeros((head_count, HD, HD), jnp.float32)
    transfer, _ = run_states(
        identity, key_blocks, householder_keys, jnp.zeros_like(householder_values)
    )
    offset, _ = run_states(no_state, key_blocks, householder_keys, householder_values)
    incoming = no_state
    for step_index in range(lax.axis_size("seq") - 1):
        incoming = from_behind(apply_map(transfer, incoming, offset), "seq", 1)
    (gated_rows, end_state), finish_back = jax.vjp(
        finish,
        incoming,
        query_blocks,
        key_blocks,
        householder_keys,
        householder_values,
        gate_pre,
        out_gain,
    )
    gated_low = gated_rows.astype(jnp.bfloat16)
    attn_out = lax.psum(jnp.dot(gated_low, w_o, preferred_element_type=jnp.float32), "head")
    hidden_state = tok_rows + attn_out
    normed_mlp = rms_scale(hidden_state, mlp_gain).astype(jnp.bfloat16)
    gate_up = jnp.einsum("td,cdf->tcf", normed_mlp, w_gateup, preferred_element_type=jnp.float32)
    gate_act = gate_up[:, 0]
    up_act = gate_up[:, 1]
    sig_gate = jax.nn.sigmoid(gate_act)
    silu_gate = gate_act * sig_gate
    hidden_units = (silu_gate * up_act).astype(jnp.bfloat16)
    mlp_out = lax.psum(jnp.dot(hidden_units, w_down, preferred_element_type=jnp.float32), "head")
    result = (hidden_state + mlp_out).astype(jnp.bfloat16)
    grad_rows = cotangent[0]
    grad_down = jnp.einsum("tf,td->fd", hidden_units, grad_rows, preferred_element_type=jnp.float32)
    d_hidden = jnp.einsum("td,fd->tf", grad_rows, w_down, preferred_element_type=jnp.float32)
    d_gate_act = d_hidden * up_act * (sig_gate + silu_gate * (1.0 - sig_gate))
    d_up_act = d_hidden * silu_gate
    d_gate_up = jnp.stack([d_gate_act, d_up_act], axis=1).astype(jnp.bfloat16)
    grad_gateup = jnp.einsum(
        "td,tcf->cdf", normed_mlp, d_gate_up, preferred_element_type=jnp.float32
    )
    d_normed_mlp = lax.psum(
        jnp.einsum("tcf,cdf->td", d_gate_up, w_gateup, preferred_element_type=jnp.float32), "head"
    )
    _, mlp_norm_back = jax.vjp(rms_scale, hidden_state, mlp_gain)
    d_hidden_part, grad_mlp_gain = mlp_norm_back(d_normed_mlp)
    d_hidden_state = grad_rows.astype(jnp.float32) + d_hidden_part
    d_attn_low = d_hidden_state.astype(jnp.bfloat16)
    grad_o = jnp.einsum("tc,td->cd", gated_low, d_attn_low, preferred_element_type=jnp.float32)
    d_gated = jnp.einsum("td,cd->tc", d_attn_low, w_o, preferred_element_type=jnp.float32)

    def gated_from(start_state):
        return finish(
            start_state,
            query_blocks,
            key_blocks,
            householder_keys,
            householder_values,
            gate_pre,
            out_gain,
        )[0]

    _, start_back = jax.vjp(gated_from, incoming)
    local_grad = start_back(d_gated)[0]
    transfer_t = jnp.swapaxes(transfer, 1, 2)
    outgoing = no_state
    for step_index in range(lax.axis_size("seq") - 1):
        outgoing = from_behind(apply_map(transfer_t, outgoing, local_grad), "seq", -1)
    finish_grads = finish_back((d_gated, outgoing))
    d_ext, grad_conv, d_beta_logit = prep_back(finish_grads[1:5])
    d_gate_pre = finish_grads[5]
    grad_out_gain_part = finish_grads[6]
    rim_back = from_behind(d_ext[:rim_width], "seq", -1)
    d_raw = d_ext[rim_width:] + jnp.concatenate(
        [jnp.zeros((count_rows - rim_width,) + rim_back.shape[1:], jnp.float32), rim_back], axis=0
    )
    d_projected = jnp.concatenate([d_raw, d_gate_pre[:, None]], axis=1).astype(jnp.bfloat16)
    d_beta_low = d_beta_logit.astype(jnp.bfloat16)
    grad_qkvg = jnp.einsum(
        "td,tce->cde", normed_low, d_projected, preferred_element_type=jnp.float32
    )
    grad_beta = jnp.einsum("td,th->dh", normed_low, d_beta_low, preferred_element_type=jnp.float32)
    d_normed_part = jnp.einsum(
        "tce,cde->td", d_projected, w_qkvg, preferred_element_type=jnp.float32
    ) + jnp.einsum("th,dh->td", d_beta_low, w_beta, preferred_element_type=jnp.float32)
    norm_part = jnp.sum(jnp.sqrt(jnp.sum(end_state * end_state, axis=(1, 2))))
    d_normed, out_gain_head, norm_head = lax.psum(
        (d_normed_part, grad_out_gain_part, norm_part), "head"
    )
    _, attn_norm_back = jax.vjp(rms_scale, tok_rows, attn_gain)
    d_tok_part, grad_attn_gain = attn_norm_back(d_normed)
    d_tokens = (d_hidden_state + d_tok_part).astype(jnp.bfloat16)
    small_sums = lax.psum(
        (grad_attn_gain, grad_mlp_gain, out_gain_head, grad_conv, grad_beta, norm_head),
        ("dp", "seq"),
    )
    sum_qkvg, sum_gateup, sum_o, sum_down = (
        lax.psum_scatter(grad_qkvg, ("dp", "seq"), scatter_dimension=1, tiled=True),
        lax.psum_scatter(grad_gateup, ("dp", "seq"), scatter_dimension=1, tiled=True),
        lax.psum_scatter(grad_o, ("dp", "seq"), scatter_dimension=1, tiled=True),
        lax.psum_scatter(grad_down, ("dp", "seq"), scatter_dimension=1, tiled=True),
    )
    state_mean = small_sums[5] / (lax.axis_size("dp") * lax.axis_size("seq") * H)
    return (
        result[None],
        d_tokens[None],
        small_sums[0],
        sum_qkvg,
        small_sums[4],
        small_sums[3],
        small_sums[2],
        sum_o,
        small_sums[1],
        sum_gateup,
        sum_down,
        state_mean,
    )


def solution(mesh):
    placed = (
        P("dp", "seq", None),
        P(),
        P(None, None, "head"),
        P(None, "head"),
        P(None, None, "head"),
        P(),
        P("head", None),
        P(),
        P(None, None, "head"),
        P("head", None),
        P("dp", "seq", None),
    )
    return jax.shard_map(
        per_device,
        mesh=mesh,
        in_specs=placed,
        out_specs=(
            P("dp", "seq", None),
            P("dp", "seq", None),
            P(),
            P(None, ("dp", "seq"), "head"),
            P(None, "head"),
            P(None, None, "head"),
            P(),
            P("head", ("dp", "seq")),
            P(),
            P(None, ("dp", "seq"), "head"),
            P("head", ("dp", "seq")),
            P(),
        ),
        check_vma=False,
    )
```

profile of v0, /device:TPU:0, one launch (start us, length us, event | category | flops | bytes accessed | tf_op | source)
XLA Modules:
  0.0 1606.8 jit_solution(2863792706708520678)
XLA Ops:
  10.1 10.7 fusion.214
  53.9 158.7 %custom-call.12 = f32[8,4,1,64,64]{3,4,2,1,0:T(8,128)} custom-call(f32[8,4,1,64,64]{4,3,2,1,0:T(8,128)} %fusion.114), custom_call_target="InvertDiagBlocksLowerTriangular" | custom-call | tf_op jit(solution)/shard_map/jvp(jit(_solve_triangular))/vmap(vmap())/triangular_solve | solution.py:53
  222.7 28.8 %while.86 = (s32[]{:T(128)}, f32[4,128,128]{2,1,0:T(8,128)}, f32[8,4,64,128]{3,2,1,0:T(8,128)S(1)}, f32[8,4,64,128]{3,2,1,0:T(8,128)}, f32[8,4,64,128]{3,2,1,0:T(8,128)}, /*index=5*/s32[]{:T(128)}, s32[]{:T(128)}) while((s32[]{:T(128)}, f32[4,128,128]{2,1,0:T(8,128)}, f32[8,4,64,128]{3,2,1,0:T(8,128)S(1)}, ...), condition=%wide.region_6.8_spmd.clone, body=%wide.region_5.7_spmd.clone.sunk | while | flops 100892672 | bytes 1443427 | solution.py:75
  251.5 15.3 while.82
  277.0 26.7 %while.83 = (s32[]{:T(128)}, f32[4,128,128]{2,1,0:T(8,128)S(1)}, f32[8,4,128,128]{3,2,1,0:T(8,128)}, f32[8,4,64,128]{3,2,1,0:T(8,128)}, f32[8,4,64,128]{3,2,1,0:...) while((s32[]{:T(128)}, f32[4,128,128]{2,1,0:T(8,128)S(1)}, ...), condition=%wide.region_8.10_spmd, body=%wide.region_7.9_spmd.sunk | while | flops 100761600 | bytes 2098277 | solution.py:75
  328.2 152.2 %all-reduce.20.cloned.1.call-done = f32[512,2048]{1,0:T(8,128)} async-done(((f32[512,2048]{1,0:T(8,128)}), f32[512,2048]{1,0:T(8,128)}) %all-reduce.20.cloned.1.call-update) | async-done | bytes 4194320 | tf_op jit(solution)/shard_map/psum | solution.py:146
  486.0 11.5 fusion.180
  497.6 7.0 fusion.91
  505.6 8.9 convolution_bitcast_fusion.4
  516.1 21.6 %while.84 = (s32[]{:T(128)}, f32[4,128,128]{2,1,0:T(8,128)S(1)}, f32[8,4,128,128]{3,2,1,0:T(8,128)}, f32[8,4,64,128]{3,2,1,0:T(8,128)S(1)}, f32[8,4,64,128]{3,2,...) while((s32[]{:T(128)}, f32[4,128,128]{2,1,0:T(8,128)S(1)}, f32[8,4,128,128]{3,2,1,0:T(8,128)}, ...), condition=%wide.region_17.19_spmd, body=%wide.region_16.18_spmd.sunk | while | flops 100761600 | bytes 1967197 | solution.py:75
  544.3 8.0 fusion.92
  552.3 116.4 %all-reduce.22.cloned.1.call-done = f32[512,2048]{1,0:T(8,128)} async-done(((f32[512,2048]{1,0:T(8,128)}), f32[512,2048]{1,0:T(8,128)}) %all-reduce.22.cloned.1.call-update) | async-done | bytes 4194320 | tf_op jit(solution)/shard_map/psum | solution.py:166
  717.5 15.6 while.87
  771.7 55.9 %while.85 = (s32[]{:T(128)}, f32[4,128,128]{2,1,0:T(8,128)S(1)}, f32[8,4,64,128]{3,2,1,0:T(8,128)}, f32[8,4,64,128]{3,2,1,0:T(8,128)}, f32[8,4,64,128]{3,2,1,0:T...) while((s32[]{:T(128)}, f32[4,128,128]{2,1,0:T(8,128)S(1)}, ...), condition=%wide.region_23.25_spmd, body=%wide.region_22.24_spmd.sunk | while | flops 201523200 | bytes 2756745 | solution.py:75
  895.3 9.6 convolution_bitcast_fusion.3
  906.3 12.9 convolution_bitcast_fusion.2
  927.4 8.8 fusion.77
  937.8 10.9 all-reduce.13
  951.0 233.7 %all-reduce.24.cloned.1.call-done = (f32[512,2048]{1,0:T(8,128)}, f32[512,2048]{1,0:T(8,128)}) async-done(((f32[512,2048]{1,0:T(8,128)}, f32[512,2048]{1,0:T(8,128)}), (f32[512,2048]{1,0:T(8,128)}, f32[512,2048]{1,0:T(8,128)})) %all-reduce.24.cloned.1.call-update) | async-done | bytes 8388624 | tf_op jit(solution)/shard_map/psum | solution.py:155
  1189.0 25.4 %all-reduce.25 = (f32[2048]{0:T(1024)}, f32[2048,4]{0,1:T(4,128)}, f32[3,4,512]{2,0,1:T(4,128)S(1)}, f32[128]{0:T(128)}, f32[2048]{0:T(1024)}, /*index=5*/f32[]{:T(128)}) all-reduce(f32[2048]{0:T(1024)S(1)} %get-tuple-element.563, f32[2048,4]{0,1:T(4,128)S(1)} %fusion.206, ...), channel_id=1, replica_groups=mesh['dp'=4,'seq'=2,'head'=4] {'dp','seq'}, use_global_device_ids=true, to_apply=%region_31.34 | all-reduce | flops 18561 | bytes 148488 | tf_op jit(solution)/shard_map/psum | solution.py:217
  1225.4 77.8 %reduce-scatter.5.cloned.1.call-done = f32[4,256,512]{1,2,0:T(8,128)} async-done(((f32[4,2048,512]{1,2,0:T(8,128)}), f32[4,256,512]{1,2,0:T(8,128)}) %reduce-scatter.5.cloned.1.call-update) | async-done | bytes 2097168 | tf_op jit(solution)/shard_map/reduce_scatter | solution.py:222
  1306.2 146.5 %reduce-scatter.9.cloned.1.call-done = f32[2,256,1408]{1,2,0:T(8,128)} async-done(((f32[2,2048,1408]{1,2,0:T(8,128)}), f32[2,256,1408]{1,2,0:T(8,128)}) %reduce-scatter.9.cloned.1.call-update) | async-done | bytes 2883600 | tf_op jit(solution)/shard_map/reduce_scatter | solution.py:223
  1456.1 51.5 %reduce-scatter.7.cloned.1.call-done = f32[512,256]{1,0:T(8,128)} async-done(((f32[512,2048]{1,0:T(8,128)}), f32[512,256]{1,0:T(8,128)}) %reduce-scatter.7.cloned.1.call-update) | async-done | bytes 524304 | tf_op jit(solution)/shard_map/reduce_scatter | solution.py:224
  1507.6 91.0 %reduce-scatter.11.cloned.1.call-done = f32[1408,256]{1,0:T(8,128)} async-done(((f32[1408,2048]{1,0:T(8,128)}), f32[1408,256]{1,0:T(8,128)}) %reduce-scatter.11.cloned.1.call-update) | async-done | bytes 1441808 | tf_op jit(solution)/shard_map/reduce_scatter | solution.py:225
  (521 shorter events, 446.5 us)
Async XLA Ops:
  7.2 312.6 %copy-start = (bf16[512,2048]{1,0:T(8,128)(2,1)S(1)}, bf16[512,2048]{1,0:T(8,128)(2,1)}, u32[]{:S(2)}) copy-start(bf16[512,2048]{1,0:T(8,128)(2,1)} %param.35) | copy-start | bytes 6291460
  7.2 473.2 %all-reduce.20.cloned.1.call-start = ((), (), s32[]{:S(2)}) async-start(), calls=%async_computation.4 | async-start | bytes 8388608 | tf_op jit(solution)/shard_map/psum | solution.py:146
  10.0 13.8 copy-start.94
  10.1 13.8 copy-start.23
  10.1 13.8 copy-start.85
  10.1 13.8 copy-start.100
  20.8 6.6 collective-permute-start
  268.2 5.4 collective-permute-start.1
  323.2 345.4 %all-reduce.22.cloned.1.call-start = ((), (), s32[]{:S(2)}) async-start(), calls=%async_computation.5 | async-start | bytes 8388608 | tf_op jit(solution)/shard_map/psum | solution.py:166
  328.2 157.7 %copy-start.89 = (f32[2048]{0:T(1024)S(1)}, f32[2048]{0:T(1024)}, u32[]{:S(2)}) copy-start(f32[2048]{0:T(1024)} %param.36) | copy-start | bytes 24580
  480.4 17.1 %slice-start.3 = ((s8[5767168]{0:T(1024)(128)(4,1)}), s8[4194304]{0:T(1024)(128)(4,1)S(1)}, s32[]{:S(2)}) async-start(s8[5767168]{0:T(1024)(128)(4,1)} %bitcast.465), calls=%async_computation.14 | async-start | bytes 8388608
  484.1 189.8 %copy-start.98 = (f32[512]{0:T(512)}, f32[512]{0:T(512)S(1)}, u32[]{:S(2)}) copy-start(f32[512]{0:T(512)S(1)} %fusion.190) | copy-start | bytes 6148
  486.0 19.6 %slice-start = ((s8[11534336]{0:T(1024)(128)(4,1)}), s8[4194304]{0:T(1024)(128)(4,1)S(1)}, s32[]{:S(2)}) async-start(s8[11534336]{0:T(1024)(128)(4,1)} %bitcast.463), calls=%async_computation.11 | async-start | bytes 8388608
  486.0 19.6 %slice-start.1 = ((s8[11534336]{0:T(1024)(128)(4,1)}), s8[4194304]{0:T(1024)(128)(4,1)S(1)}, s32[]{:S(2)}) async-start(s8[11534336]{0:T(1024)(128)(4,1)} %bitcast.463), calls=%async_computation.12 | async-start | bytes 8388608
  514.5 670.2 %all-reduce.24.cloned.1.call-start = ((), (), s32[]{:S(2)}) async-start(), calls=%async_computation.10 | async-start | bytes 16777216 | tf_op jit(solution)/shard_map/psum | solution.py:155
  717.5 15.6 copy-start.17
  733.7 34.6 %collective-permute-start.2 = (f32[4,128,128]{2,1,0:T(8,128)S(1)}, f32[4,128,128]{2,1,0:T(8,128)S(1)}, u32[]{:S(2)}, u32[]{:S(2)}) collective-permute-start(f32[4,128,128]{2,1,0:T(8,128)S(1)} %convolution_add_fusion.13), channel_id=1, source_target_pairs={{4,0},{5,1},{6,2},{7,3},{12,8},{13,9},{14,10},{15,11},{20,16},{21,... | collective-permute-start | bytes 786440 | tf_op jit(solution)/shard_map/ppermute | solution.py:17
  875.2 7.9 collective-permute-start.3
  893.8 409.4 %reduce-scatter.5.cloned.1.call-start = ((), (), s32[]{:S(2)}) async-start(), calls=%async_computation.6 | async-start | bytes 18874368 | tf_op jit(solution)/shard_map/reduce_scatter | solution.py:222
  905.0 547.8 %reduce-scatter.9.cloned.1.call-start = ((), (), s32[]{:S(2)}) async-start(), calls=%async_computation.8 | async-start | bytes 25952256 | tf_op jit(solution)/shard_map/reduce_scatter | solution.py:223
  919.3 588.3 %reduce-scatter.7.cloned.1.call-start = ((), (), s32[]{:S(2)}) async-start(), calls=%async_computation.7 | async-start | bytes 4718592 | tf_op jit(solution)/shard_map/reduce_scatter | solution.py:224
  925.8 672.7 %reduce-scatter.11.cloned.1.call-start = ((), (), s32[]{:S(2)}) async-start(), calls=%async_computation.9 | async-start | bytes 12976128 | tf_op jit(solution)/shard_map/reduce_scatter | solution.py:225
  1184.7 30.8 %copy-start.97 = (f32[512]{0:T(512)S(1)}, f32[512]{0:T(512)}, u32[]{:S(2)}) copy-start(f32[512]{0:T(512)} %copy-done.96) | copy-start | bytes 6148
  1303.2 295.4 %copy-start.1 = (bf16[512,2048]{1,0:T(8,128)(2,1)S(1)}, bf16[512,2048]{1,0:T(8,128)(2,1)}, u32[]{:S(2)}) copy-start(bf16[512,2048]{1,0:T(8,128)(2,1)} %param.35) | copy-start | bytes 6291460
  (100 other events, 429.8 us)
Sparse Core Ops, SparseCore 0:
  323.3 157.0 all-reduce.19
  514.7 153.9 all-reduce.21
  893.9 290.8 all-reduce.23
  1188.2 114.9 reduce-scatter.4
  1306.6 146.0 reduce-scatter.8
  1456.5 51.0 reduce-scatter.6
  1511.7 86.8 reduce-scatter.10
where the time goes:
time: 1610 us
  waiting for transfers between devices  869 us (54%)
  matrix products  349 us (22%)
  other arithmetic  219 us (14%)
  local copies, waits for them, and re-layouts  107 us (7%)
  blocking collectives  36.3 us (2%)
  between operations  17.5 us (1%)
    psum x1, waiting for transfers between devices, per_device(): lax.psum(jnp.dot(hidden_units, w_down, preferred_element_type=jnp.float32...  234 us
    another operation x4, other arithmetic, prepare(): jax.scipy.linalg.solve_triangular(system, scaled, lower=True, unit_diagon...  160 us
    psum x1, waiting for transfers between devices, per_device(): lax.psum(jnp.dot(gated_low, w_o, preferred_element_type=jnp.float32), 'he...  152 us
    reduce_scatter x1, waiting for transfers between devices, per_device(): lax.psum_scatter(grad_gateup, ('dp', 'seq'), scatter_dimension=1, tiled=T...  147 us
    psum x1, waiting for transfers between devices, per_device(): lax.psum(jnp.einsum('tcf,cdf->td', d_gate_up, w_gateup, preferred_element...  116 us
    reduce_scatter x1, waiting for transfers between devices, per_device(): lax.psum_scatter(grad_down, ('dp', 'seq'), scatter_dimension=1, tiled=True)  91 us
    dot_general x56, matrix products, advance(): jnp.einsum('nij,njq->niq', weighted_keys, running_state, precision=FULL_P...  90.5 us
    reduce_scatter x1, waiting for transfers between devices, per_device(): lax.psum_scatter(grad_qkvg, ('dp', 'seq'), scatter_dimension=1, tiled=True)  77.8 us
  transfers between devices with their start and end apart: 11, of which 7 were waited for; matrix products, arithmetic and copies ran while one was open for 9% of the time, Pallas kernels for 0%

commit v1 on v0

v1 whole, which is shorter than its diff:
```python
import functools

import jax
import jax.numpy as jnp
from jax import lax
from jax.experimental import pallas as pl
from jax.experimental.pallas import tpu as pltpu
from jax.sharding import PartitionSpec as P

HD = 128
SPAN = 64
RIM = 16


MESH_ID = pl.DeviceIdType.MESH
F32 = jnp.float32
BF = jnp.bfloat16


def dot_nn(a, b):
    return lax.dot_general(a, b, (((1,), (0,)), ((), ())), preferred_element_type=F32)


def dot_nt(a, b):
    return lax.dot_general(a, b, (((1,), (1,)), ((), ())), preferred_element_type=F32)


def dot_tn(a, b):
    return lax.dot_general(a, b, (((0,), (0,)), ((), ())), preferred_element_type=F32)


def halves(a):
    high = a.astype(BF)
    return high, (a - high.astype(F32)).astype(BF)


def dot_fine(a, b, dot=dot_nn):
    a_high, a_rest = halves(a)
    b_high, b_rest = halves(b)
    return dot(a_high, b_high) + (dot(a_high, b_rest) + dot(a_rest, b_high))


def stack_heads(x, heads):
    return jnp.concatenate([x[:, h * HD : (h + 1) * HD] for h in range(heads)], axis=0)


def spread_heads(x, heads):
    return jnp.concatenate([x[h * SPAN : (h + 1) * SPAN] for h in range(heads)], axis=1)


def stack_column(x, heads):
    return jnp.concatenate(
        [jnp.broadcast_to(x[:, h : h + 1], (SPAN, HD)) for h in range(heads)], axis=0
    )


def sigmoid(x):
    return 1.0 / (1.0 + jnp.exp(-x))


def rows_of(b, count=SPAN):
    return pl.ds(pl.multiple_of(b * SPAN, SPAN), count)


def raw_window(raw, rim, c, b):
    now = raw[c, rows_of(b), :].astype(F32)
    start = pl.multiple_of(jnp.maximum(b * SPAN - RIM, 0), RIM)
    before = jnp.where(b == 0, rim[c].astype(F32), raw[c, pl.ds(start, RIM), :].astype(F32))
    return jnp.concatenate([before[RIM - 8 :], now], axis=0)


def shifted(window, j, taps):
    start = 8 - (taps - 1) + j
    return window[start : start + SPAN]


def meet(idx, count, axis):
    barrier = pltpu.get_barrier_semaphore()

    @pl.when(idx > 0)
    def _():
        pl.semaphore_signal(barrier, inc=1, device_id={axis: idx - 1}, device_id_type=MESH_ID)

    @pl.when(idx < count - 1)
    def _():
        pl.semaphore_signal(barrier, inc=1, device_id={axis: idx + 1}, device_id_type=MESH_ID)

    @pl.when(idx > 0)
    def _():
        pl.semaphore_wait(barrier, 1)

    @pl.when(idx < count - 1)
    def _():
        pl.semaphore_wait(barrier, 1)


def send_to(src, dst, send_sem, recv_sem, axis, target):
    return pltpu.make_async_remote_copy(
        src_ref=src,
        dst_ref=dst,
        send_sem=send_sem,
        recv_sem=recv_sem,
        device_id={axis: target},
        device_id_type=MESH_ID,
    )


def block_masks(heads):
    side = heads * SPAN
    row = lax.broadcasted_iota(jnp.int32, (side, side), 0)
    col = lax.broadcasted_iota(jnp.int32, (side, side), 1)
    same = (row // SPAN) == (col // SPAN)
    return row, col, same & (row > col), same & (row >= col)


def unit_lower_inverse(lower, row, col):
    inverse = jnp.where(row == col, 1.0, 0.0) - jnp.where((row // 2) == (col // 2), lower, 0.0)
    m = 2
    while m < SPAN:
        off = jnp.where(((row // (2 * m)) == (col // (2 * m))) & ((row // m) != (col // m)), lower, 0.0)
        inverse = inverse - dot_fine(dot_fine(inverse, off), inverse)
        m *= 2
    return inverse


def delta_forward_kernel(
    heads, runs, raw, conv_w, beta, gate, gain,
    gated, q_s, k_s, w_s, u_s, t_s, p_s, f_s, s_s, o_s, rim, norm,
    u_full, state, state_in, rim_in, rim_sems, state_sems,
):
    idx = lax.axis_index("seq")
    count_rows = raw.shape[1]
    taps = conv_w.shape[1]
    blocks = count_rows // SPAN
    last = count_rows - RIM
    if runs > 1:
        meet(idx, runs, "seq")

        @pl.when(idx < runs - 1)
        def _():
            send_to(raw.at[:, pl.ds(last, RIM), :], rim_in, rim_sems.at[0], rim_sems.at[1], "seq", idx + 1).start()

    row, col, strict, causal = block_masks(heads)

    def prepare_group(g, group):
        @pl.when(g == 0)
        def _():
            @pl.when(idx == 0)
            def _():
                rim[...] = jnp.zeros_like(rim)

            if runs > 1:
                @pl.when(idx > 0)
                def _():
                    send_to(rim_in, rim_in, rim_sems.at[0], rim_sems.at[1], "seq", idx - 1).wait_recv()
                    rim[...] = rim_in[...]

        for part in range(group):
            b = g * group + part
            parts = []
            for c in range(3):
                window = raw_window(raw, rim, c, b)
                taps_c = conv_w[c]
                mixed = taps_c[0:1] * shifted(window, 0, taps)
                for j in range(1, taps):
                    mixed = mixed + taps_c[j : j + 1] * shifted(window, j, taps)
                parts.append(stack_heads(mixed * sigmoid(mixed), heads))
            q, k, v = parts
            q = q * (lax.rsqrt(jnp.sum(q * q, axis=1, keepdims=True) + 1e-06) * HD ** (-0.5))
            k = k * lax.rsqrt(jnp.sum(k * k, axis=1, keepdims=True) + 1e-06)
            beta_c = stack_column(beta[rows_of(b), :], heads)
            scaled = k * beta_c
            lower = jnp.where(strict, dot_fine(scaled, k, dot_nt), 0.0)
            inverse = unit_lower_inverse(lower, row, col).astype(BF)
            k_low = k.astype(BF)
            q_low = q.astype(BF)
            wu = dot_nn(inverse, jnp.concatenate([scaled, v * beta_c], axis=1).astype(BF))
            attention = jnp.where(causal, dot_nt(q_low, k_low), 0.0)
            q_s[b] = q_low
            k_s[b] = k_low
            t_s[b] = inverse
            p_s[b] = attention.astype(BF)
            w_s[b] = wu[:, :HD].astype(BF)
            u_full[b] = wu[:, HD:]
            u_s[b] = wu[:, HD:].astype(BF)

    group = 2
    groups = blocks // group

    def prepare_loop(i, carry):
        prepare_group(groups - 1 - i, group)
        return carry

    lax.fori_loop(0, groups, prepare_loop, 0)

    @pl.when(idx == 0)
    def _():
        state[...] = jnp.zeros_like(state)

    if runs > 1:
        @pl.when(idx > 0)
        def _():
            send_to(state_in, state_in, state_sems.at[0], state_sems.at[1], "seq", idx - 1).wait_recv()
            state[...] = state_in[...]

    gain_row = gain[...]

    def scan_block(b, carry):
        fresh, out_part = [], []
        before = [state[h] for h in range(heads)]
        for h in range(heads):
            mine = pl.ds(h * SPAN, SPAN)
            low = before[h].astype(BF)
            s_s[b, h] = low
            both = dot_nn(jnp.concatenate([w_s[b, mine, :], q_s[b, mine, :]], axis=0), low)
            fresh.append(u_full[b, mine, :] - both[:SPAN])
            out_part.append(both[SPAN:])
        for h in range(heads):
            mine = pl.ds(h * SPAN, SPAN)
            state[h] = before[h] + dot_tn(k_s[b, mine, :], fresh[h].astype(BF))
        fresh_low = jnp.concatenate(fresh, axis=0).astype(BF)
        f_s[b] = fresh_low
        out = jnp.concatenate(out_part, axis=0) + dot_nn(p_s[b], fresh_low)
        o_s[b] = out
        g = stack_heads(gate[rows_of(b), :], heads)
        scale = lax.rsqrt(jnp.mean(out * out, axis=1, keepdims=True) + 1e-05)
        gated[rows_of(b), :] = spread_heads(out * scale * gain_row * (g * sigmoid(g)), heads).astype(BF)
        return carry

    lax.fori_loop(0, blocks, scan_block, 0)
    if runs > 1:
        @pl.when(idx < runs - 1)
        def _():
            send_to(state, state_in, state_sems.at[0], state_sems.at[1], "seq", idx + 1).start()

    total = jnp.zeros((1, HD), F32)
    for h in range(heads):
        end = state[h]
        square = jnp.sum(jnp.sum(end * end, axis=0, keepdims=True), axis=1, keepdims=True)
        total = total + jnp.broadcast_to(jnp.sqrt(square), (1, HD))
    norm[...] = jnp.broadcast_to(total, norm.shape)
    if runs > 1:
        @pl.when(idx < runs - 1)
        def _():
            send_to(raw.at[:, pl.ds(last, RIM), :], rim_in, rim_sems.at[0], rim_sems.at[1], "seq", idx + 1).wait_send()
            send_to(state, state_in, state_sems.at[0], state_sems.at[1], "seq", idx + 1).wait_send()


def delta_forward(raw, conv_w, beta, gate, gain, runs):
    count_rows, heads = beta.shape
    blocks = count_rows // SPAN
    side = heads * SPAN
    width = heads * HD
    sd = jax.ShapeDtypeStruct
    outs = [
        sd((count_rows, width), BF),
        sd((blocks, side, HD), BF),
        sd((blocks, side, HD), BF),
        sd((blocks, side, HD), BF),
        sd((blocks, side, HD), BF),
        sd((blocks, side, side), BF),
        sd((blocks, side, side), BF),
        sd((blocks, side, HD), BF),
        sd((blocks, heads, HD, HD), BF),
        sd((blocks, side, HD), F32),
        sd((3, RIM, width), BF),
        sd((8, HD), F32),
    ]
    vmem = pl.BlockSpec(memory_space=pltpu.VMEM)
    return pl.pallas_call(
        functools.partial(delta_forward_kernel, heads, runs),
        out_shape=outs,
        in_specs=[vmem] * 5,
        out_specs=[vmem] * len(outs),
        scratch_shapes=[
            pltpu.VMEM((blocks, side, HD), F32),
            pltpu.VMEM((heads, HD, HD), F32),
            pltpu.VMEM((heads, HD, HD), F32),
            pltpu.VMEM((3, RIM, width), BF),
            pltpu.SemaphoreType.DMA((2,)),
            pltpu.SemaphoreType.DMA((2,)),
        ],
        compiler_params=pltpu.CompilerParams(
            collective_id=0 if runs > 1 else None, has_side_effects=True, vmem_limit_bytes=48 << 20
        ),
        name="delta_forward",
    )(raw, conv_w, beta, gate, gain.reshape(1, HD))


def delta_backward_kernel(
    heads, runs, raw, rim, conv_w, beta, gate, gain,
    q_s, k_s, w_s, u_s, t_s, p_s, f_s, s_s, o_s, d_gated,
    d_raw, d_gate, d_beta, g_conv, g_gain,
    d_mixed, d_out, d_fresh, d_fresh0, q_out, after_s, state, state_in, edge_in, conv_acc, gain_acc,
    state_sems, edge_sems,
):
    idx = lax.axis_index("seq")
    count_rows = raw.shape[1]
    taps = conv_w.shape[1]
    blocks = count_rows // SPAN
    if runs > 1:
        meet(idx, runs, "seq")
    gain_row = gain[...]
    gain_acc[...] = jnp.zeros_like(gain_acc)
    conv_acc[...] = jnp.zeros_like(conv_acc)

    def gate_block(b, carry):
        o = o_s[b]
        g = stack_heads(gate[rows_of(b), :], heads)
        dg = stack_heads(d_gated[rows_of(b), :].astype(F32), heads)
        scale = lax.rsqrt(jnp.mean(o * o, axis=1, keepdims=True) + 1e-05)
        y = o * scale
        sig = sigmoid(g)
        silu = g * sig
        dgy = dg * y
        gain_acc[...] += jnp.sum((dgy * silu).reshape(-1, 8, HD), axis=0)
        d_gate[rows_of(b), :] = spread_heads(dgy * gain_row * (sig + silu * (1.0 - sig)), heads).astype(BF)
        dy = dg * gain_row * silu
        do = (scale * (dy - y * jnp.mean(dy * y, axis=1, keepdims=True))).astype(BF)
        d_out[b] = do
        d_fresh0[b] = dot_tn(p_s[b], do)
        for h in range(heads):
            mine = slice(h * SPAN, (h + 1) * SPAN)
            q_out[b, h] = dot_tn(q_s[b, mine, :], do[mine])
        return carry

    lax.fori_loop(0, blocks, gate_block, 0)

    @pl.when(idx == runs - 1)
    def _():
        state[...] = jnp.zeros_like(state)

    if runs > 1:
        @pl.when(idx < runs - 1)
        def _():
            send_to(state_in, state_in, state_sems.at[0], state_sems.at[1], "seq", idx + 1).wait_recv()
            state[...] = state_in[...]

    def scan_block(i, carry):
        b = blocks - 1 - i
        for h in range(heads):
            mine = pl.ds(h * SPAN, SPAN)
            after = state[h]
            low = after.astype(BF)
            after_s[b, h] = low
            df = (d_fresh0[b, mine, :] + dot_nn(k_s[b, mine, :], low)).astype(BF)
            d_fresh[b, mine, :] = df
            state[h] = after + q_out[b, h] - dot_tn(w_s[b, mine, :], df)
        return carry

    lax.fori_loop(0, blocks, scan_block, 0)
    if runs > 1:
        @pl.when(idx > 0)
        def _():
            send_to(state, state_in, state_sems.at[0], state_sems.at[1], "seq", idx - 1).start()

    row, col, strict, causal = block_masks(heads)
    lane = lax.broadcasted_iota(jnp.int32, (SPAN, HD), 1)

    def grad_block(b, carry):
        df = d_fresh[b]
        do = d_out[b]
        k_low = k_s[b]
        dw, dq, dk = [], [], []
        for h in range(heads):
            mine = slice(h * SPAN, (h + 1) * SPAN)
            both = dot_nt(jnp.concatenate([df[mine], do[mine]], axis=0), s_s[b, h])
            dw.append(-both[:SPAN])
            dq.append(both[SPAN:])
            dk.append(dot_nt(f_s[b, mine, :], after_s[b, h]))
        dw = jnp.concatenate(dw, axis=0)
        dp = jnp.where(causal, dot_nt(do, f_s[b]), 0.0).astype(BF)
        dq = jnp.concatenate(dq, axis=0) + dot_nn(dp, k_low)
        dk = jnp.concatenate(dk, axis=0) + dot_tn(dp, q_s[b])
        dx = dot_tn(t_s[b], jnp.concatenate([dw.astype(BF), df], axis=1))
        wu = jnp.concatenate([w_s[b], u_s[b]], axis=1)
        dl = jnp.where(strict, -dot_nt(dx.astype(BF), wu), 0.0).astype(BF)
        d_scaled = dx[:, :HD] + dot_nn(dl, k_low)
        d_vb = dx[:, HD:]
        beta_rows = beta[rows_of(b), :]
        beta_c = stack_column(beta_rows, heads)

        windows, mixed, sigs, acts = [], [], [], []
        for c in range(3):
            window = raw_window(raw, rim, c, b)
            taps_c = conv_w[c]
            m = taps_c[0:1] * shifted(window, 0, taps)
            for j in range(1, taps):
                m = m + taps_c[j : j + 1] * shifted(window, j, taps)
            s = sigmoid(m)
            windows.append(window)
            mixed.append(m)
            sigs.append(s)
            acts.append(stack_heads(m * s, heads))
        qa, ka, va = acts
        q_scale = lax.rsqrt(jnp.sum(qa * qa, axis=1, keepdims=True) + 1e-06)
        k_scale = lax.rsqrt(jnp.sum(ka * ka, axis=1, keepdims=True) + 1e-06)
        q_unit = qa * q_scale
        k = ka * k_scale
        dk = dk + dot_tn(dl, (k * beta_c).astype(BF)) + beta_c * d_scaled
        d_beta_c = jnp.sum(d_scaled * k + d_vb * va, axis=1, keepdims=True)
        d_beta_c = jnp.broadcast_to(d_beta_c, (heads * SPAN, HD)) * beta_c * (1.0 - beta_c)
        d_beta_rows = jnp.zeros((SPAN, HD), F32)
        for h in range(heads):
            d_beta_rows = jnp.where(lane == h, d_beta_c[h * SPAN : (h + 1) * SPAN], d_beta_rows)
        d_beta[rows_of(b), :] = d_beta_rows.astype(BF)
        dq = dq * HD ** (-0.5)
        d_acts = (
            q_scale * (dq - q_unit * jnp.sum(dq * q_unit, axis=1, keepdims=True)),
            k_scale * (dk - k * jnp.sum(dk * k, axis=1, keepdims=True)),
            d_vb * beta_c,
        )
        for c in range(3):
            s, m = sigs[c], mixed[c]
            dm = spread_heads(d_acts[c], heads) * (s * (1.0 + m * (1.0 - s)))
            d_mixed[c, rows_of(b), :] = dm
            for j in range(taps):
                conv_acc[c, j] += jnp.sum((dm * shifted(windows[c], j, taps)).reshape(SPAN // 8, 8, -1), axis=0)
        return carry

    lax.fori_loop(0, blocks, grad_block, 0)
    if runs > 1:
        @pl.when(idx > 0)
        def _():
            send_to(d_mixed.at[:, pl.ds(0, 8), :], edge_in, edge_sems.at[0], edge_sems.at[1], "seq", idx - 1).start()

    for c in range(3):
        for j in range(taps):
            g_conv[c, pl.ds(j, 1), :] = jnp.sum(conv_acc[c, j], axis=0, keepdims=True)
    g_gain[...] = gain_acc[...]

    @pl.when(idx == runs - 1)
    def _():
        d_mixed[:, pl.ds(count_rows, 8), :] = jnp.zeros((3, 8, d_mixed.shape[2]), F32)

    if runs > 1:
        @pl.when(idx < runs - 1)
        def _():
            send_to(edge_in, edge_in, edge_sems.at[0], edge_sems.at[1], "seq", idx + 1).wait_recv()
            d_mixed[:, pl.ds(count_rows, 8), :] = edge_in[...]

    def raw_block(b, carry):
        for c in range(3):
            window = d_mixed[c, rows_of(b, SPAN + 8), :]
            taps_c = conv_w[c]
            total = taps_c[taps - 1 : taps] * window[:SPAN]
            for j in range(taps - 1):
                ahead = taps - 1 - j
                total = total + taps_c[j : j + 1] * window[ahead : ahead + SPAN]
            d_raw[c, rows_of(b), :] = total.astype(BF)
        return carry

    lax.fori_loop(0, blocks, raw_block, 0)
    if runs > 1:
        @pl.when(idx > 0)
        def _():
            send_to(state, state_in, state_sems.at[0], state_sems.at[1], "seq", idx - 1).wait_send()
            send_to(d_mixed.at[:, pl.ds(0, 8), :], edge_in, edge_sems.at[0], edge_sems.at[1], "seq", idx - 1).wait_send()


def delta_backward(raw, conv_w, beta, gate, gain, saved, d_gated, runs):
    count_rows, heads = beta.shape
    blocks = count_rows // SPAN
    side = heads * SPAN
    width = heads * HD
    taps = conv_w.shape[1]
    sd = jax.ShapeDtypeStruct
    q_s, k_s, w_s, u_s, t_s, p_s, f_s, s_s, o_s, rim = saved
    outs = [
        sd((3, count_rows, width), BF),
        sd((count_rows, width), BF),
        sd((count_rows, HD), BF),
        sd((3, taps, width), F32),
        sd((8, HD), F32),
    ]
    vmem = pl.BlockSpec(memory_space=pltpu.VMEM)
    return pl.pallas_call(
        functools.partial(delta_backward_kernel, heads, runs),
        out_shape=outs,
        in_specs=[vmem] * 16,
        out_specs=[vmem] * len(outs),
        scratch_shapes=[
            pltpu.VMEM((3, count_rows + 8, width), F32),
            pltpu.VMEM((blocks, side, HD), BF),
            pltpu.VMEM((blocks, side, HD), BF),
            pltpu.VMEM((blocks, side, HD), F32),
            pltpu.VMEM((blocks, heads, HD, HD), F32),
            pltpu.VMEM((blocks, heads, HD, HD), BF),
            pltpu.VMEM((heads, HD, HD), F32),
            pltpu.VMEM((heads, HD, HD), F32),
            pltpu.VMEM((3, 8, width), F32),
            pltpu.VMEM((3, taps, 8, width), F32),
            pltpu.VMEM((8, HD), F32),
            pltpu.SemaphoreType.DMA((2,)),
            pltpu.SemaphoreType.DMA((2,)),
        ],
        compiler_params=pltpu.CompilerParams(
            collective_id=1 if runs > 1 else None, has_side_effects=True, vmem_limit_bytes=56 << 20
        ),
        name="delta_backward",
    )(raw, rim, conv_w, beta, gate, gain.reshape(1, HD), q_s, k_s, w_s, u_s, t_s, p_s, f_s, s_s, o_s, d_gated)


def inverse_rms(values):
    return lax.rsqrt(jnp.mean(values * values, axis=-1, keepdims=True) + 1e-06)


def dot32(spec, a, b):
    return jnp.einsum(spec, a, b, preferred_element_type=F32)


def norm_back(values, gain, d_values):
    r = inverse_rms(values)
    e = d_values * gain
    grad_gain = jnp.sum(d_values * (values * r), axis=0)
    return r * (e - values * (r * r) * jnp.mean(e * values, axis=-1, keepdims=True)), grad_gain


def per_device(
    tokens, attn_gain, w_qkvg, w_beta, conv_w, out_gain, w_o, mlp_gain, w_gateup, w_down, cotangent
):
    runs = lax.axis_size("seq")
    everyone = ("dp", "seq")
    tok_rows = tokens[0].astype(F32)
    heads = w_beta.shape[1]
    normed = (tok_rows * inverse_rms(tok_rows) * attn_gain).astype(BF)
    projected = dot32("td,cde->cte", normed, w_qkvg)
    raw = projected[:3].astype(BF)
    gate = projected[3]
    beta = jax.nn.sigmoid(dot32("td,dh->th", normed, w_beta))
    gated, *saved = delta_forward(raw, conv_w, beta, gate, out_gain, runs)
    norm_part = saved.pop()[0, 0]
    attn = lax.psum(dot32("tc,cd->td", gated, w_o).astype(BF), "head").astype(F32)
    hidden = tok_rows + attn
    normed_mlp = (hidden * inverse_rms(hidden) * mlp_gain).astype(BF)
    gate_up = dot32("td,cdf->ctf", normed_mlp, w_gateup)
    gate_act, up_act = gate_up[0], gate_up[1]
    sig = jax.nn.sigmoid(gate_act)
    silu = gate_act * sig
    units = (silu * up_act).astype(BF)
    mlp_out = lax.psum(dot32("tf,fd->td", units, w_down).astype(BF), "head").astype(F32)
    result = (hidden + mlp_out).astype(BF)
    cot = cotangent[0]
    d_hidden = dot32("td,fd->tf", cot, w_down)
    d_gate_up = jnp.stack(
        [d_hidden * up_act * (sig + silu * (1.0 - sig)), d_hidden * silu], axis=0
    ).astype(BF)
    d_normed_mlp = lax.psum(dot32("ctf,cdf->td", d_gate_up, w_gateup).astype(BF), "head").astype(F32)
    d_hidden_part, grad_mlp_gain = norm_back(hidden, mlp_gain, d_normed_mlp)
    d_hidden_state = cot.astype(F32) + d_hidden_part
    d_attn = d_hidden_state.astype(BF)
    d_gated = dot32("td,cd->tc", d_attn, w_o)
    d_raw, d_gate, d_beta, grad_conv, grad_gain_rows = delta_backward(
        raw, conv_w, beta, gate, out_gain, saved, d_gated, runs
    )
    d_beta = d_beta[:, :heads]
    d_proj = jnp.concatenate([d_raw, d_gate[None]], axis=0)
    d_normed = lax.psum(
        (dot32("cte,cde->td", d_proj, w_qkvg) + dot32("th,dh->td", d_beta, w_beta)).astype(BF), "head"
    ).astype(F32)
    d_tok_part, grad_attn_gain = norm_back(tok_rows, attn_gain, d_normed)
    d_tokens = (d_hidden_state + d_tok_part).astype(BF)
    grad_down = dot32("tf,td->fd", units, cot).astype(BF)
    grad_gateup = dot32("td,ctf->cdf", normed_mlp, d_gate_up).astype(BF)
    grad_o = dot32("tc,td->cd", gated, d_attn).astype(BF)
    grad_qkvg = dot32("td,cte->cde", normed, d_proj).astype(BF)
    grad_beta = dot32("td,th->dh", normed, d_beta)
    out_gain_head, norm_head = lax.psum((jnp.sum(grad_gain_rows, axis=0), norm_part), "head")
    small = lax.psum(
        (grad_attn_gain, grad_mlp_gain, out_gain_head, grad_conv, grad_beta, norm_head), everyone
    )
    sum_gateup = lax.psum_scatter(grad_gateup, everyone, scatter_dimension=1, tiled=True).astype(F32)
    sum_down = lax.psum_scatter(grad_down, everyone, scatter_dimension=1, tiled=True).astype(F32)
    sum_o = lax.psum_scatter(grad_o, everyone, scatter_dimension=1, tiled=True).astype(F32)
    sum_qkvg = lax.psum_scatter(grad_qkvg, everyone, scatter_dimension=1, tiled=True).astype(F32)
    state_mean = small[5] / (lax.axis_size("dp") * runs * heads * lax.axis_size("head"))
    return (
        result[None],
        d_tokens[None],
        small[0],
        sum_qkvg,
        small[4],
        small[3],
        small[2],
        sum_o,
        small[1],
        sum_gateup,
        sum_down,
        state_mean,
    )


def solution(mesh):
    rows, halves_of = P("dp", "seq", None), P(None, None, "head")
    placed = (
        rows, P(), halves_of, P(None, "head"), halves_of, P(), P("head", None), P(),
        halves_of, P("head", None), rows,
    )
    shared = P(None, ("dp", "seq"), "head")
    turned = P("head", ("dp", "seq"))
    return jax.shard_map(
        per_device,
        mesh=mesh,
        in_specs=placed,
        out_specs=(
            rows, rows, P(), shared, P(None, "head"), halves_of, P(), turned, P(), shared, turned, P(),
        ),
        check_vma=False,
    )
```

time: 1610 us -> 742 us (0.46)
  waiting for transfers between devices: 869 us -> 471 us
  matrix products: 349 us -> 90.7 us
  other arithmetic: 219 us -> 27.8 us
  local copies, waits for them, and re-layouts: 107 us -> 21.8 us
  Pallas kernels: 0 us -> 68.4 us
    dot_general x152 -> x15, matrix products: 335 us -> 90.7 us  [dot32(): return jnp.einsum(spec, a, b, preferred_element_type=F32)]
    psum x3, waiting for transfers between devices: 502 us -> 286 us  [the longest x1 109 us: per_device(): lax.psum(dot32('tf,fd->td', units, w_down).astype(BF), 'head').astype(F32)]
    reduce_scatter x4, waiting for transfers between devices: 367 us -> 185 us  [the longest x1 87.6 us: per_device(): lax.psum_scatter(grad_gateup, everyone, scatter_dimension=1, tiled=True)]
    another operation x5 -> x0, other arithmetic: 160 us -> none  [the longest x4 160 us: prepare(): jax.scipy.linalg.solve_triangular(system, scaled, lower=True, unit_diagon...]
    pallas_call x0 -> x2, Pallas kernels: none -> 68.4 us  [the longest x1 35.1 us: delta_forward(): pl.pallas_call(functools.partial(delta_forward_kernel, heads, runs), out_...]
    unnamed x232 -> x76, local copies, waits for them, and re-layouts: 33 us -> 18.9 us
  transfers between devices with their start and end apart: 11 -> 7, of which waited for: 7 -> 6; matrix products, arithmetic and copies ran while one was open for 9% -> 9% of each run, Pallas kernels for 0% -> 5%
where the time goes in v1:
time: 742 us; the launch traced here: 734 us
  waiting for transfers between devices  471 us (63%)
  matrix products  90.7 us (12%)
  Pallas kernels  68.4 us (9%)
  blocking collectives  36.8 us (5%)
  other arithmetic  27.8 us (4%)
  local copies, waits for them, and re-layouts  21.8 us (3%)
  between operations  16.6 us (2%)
    psum x1, waiting for transfers between devices, per_device(): lax.psum(dot32('tf,fd->td', units, w_down).astype(BF), 'head').astype(F32)  109 us
    psum x1, waiting for transfers between devices, per_device(): lax.psum(dot32('tc,cd->td', gated, w_o).astype(BF), 'head').astype(F32)  92.1 us
    dot_general x15, matrix products, dot32(): return jnp.einsum(spec, a, b, preferred_element_type=F32)  90.7 us
    reduce_scatter x1, waiting for transfers between devices, per_device(): lax.psum_scatter(grad_gateup, everyone, scatter_dimension=1, tiled=True)  87.6 us
    psum x1, waiting for transfers between devices, per_device(): lax.psum(dot32('ctf,cdf->td', d_gate_up, w_gateup).astype(BF), 'head')  85.3 us
    reduce_scatter x1, waiting for transfers between devices, per_device(): lax.psum_scatter(grad_qkvg, everyone, scatter_dimension=1, tiled=True)  72.3 us
    pallas_call x1, Pallas kernels, delta_forward(): pl.pallas_call(functools.partial(delta_forward_kernel, heads, runs), out_...  35.1 us
    pallas_call x1, Pallas kernels, delta_backward(): pl.pallas_call(functools.partial(delta_backward_kernel, heads, runs), out...  33.3 us
  transfers between devices with their start and end apart: 7, of which 6 were waited for; matrix products, arithmetic and copies ran while one was open for 9% of the time, Pallas kernels for 5%

profile of v1, /device:TPU:0, one launch (start us, length us, event | category | flops | bytes accessed | tf_op | source)
XLA Modules:
  0.0 734.4 jit_solution(5070022138864410451)
XLA Ops:
  9.5 7.8 %convolution_bitcast_fusion.1 = f32[4,512,512]{2,1,0:T(8,128)S(1)} fusion(bf16[4,2048,512]{2,1,0:T(8,128)(2,1)} %param.13, bf16[1,512,2048]{2,1,0:T(8,128)(2,1)} %param.11, f32[2048]{0:T(1024)} %param.12, f32[512]{0:T(512)S(1)} %get-tuple-element.89), kind=kOutput, calls=%fused_computation.52 | convolution fusion | flops 4299161600 | bytes 14690304 | tf_op jit(solution)/shard_map/td,cde->cte/dot_general | solution.py:509
  20.6 35.1 %delta_forward.1 = (bf16[512,512]{1,0:T(8,128)(2,1)S(1)}, bf16[8,256,128]{2,1,0:T(8,128)(2,1)S(1)}, bf16[8,256,128]{2,1,0:T(8,128)(2,1)S(1)}, bf16[8,256,128]{2,...) custom-call(bf16[3,512,512]{2,1,0:T(8,128)(2,1)} %slice.64.raw, ...), custom_call_target="tpu_custom_call" | custom-call | tf_op jit(solution)/shard_map/delta_forward/pallas_call | solution.py:270
  65.1 92.1 %all-reduce.8.cloned.1.call-done = bf16[512,2048]{1,0:T(8,128)(2,1)} async-done(((bf16[512,2048]{1,0:T(8,128)(2,1)}), bf16[512,2048]{1,0:T(8,128)(2,1)}) %all-reduce.8.cloned.1.call-update) | async-done | bytes 2097168 | tf_op jit(solution)/shard_map/psum | solution.py:533
  157.2 3.1 multiply_reduce_fusion
  160.7 11.5 %convolution_bitcast_fusion = f32[2,512,1408]{2,1,0:T(8,128)} fusion(bf16[2,2048,1408]{2,1,0:T(8,128)(2,1)} %param.19, bf16[512,2048]{1,0:T(8,128)(2,1)S(1)} %copy-done.17, bf16[1,512,2048]{2,1,0:T(8,128)(2,1)S(1)} %copy-done.14, f32[2048]{0:T(1024)S(1)} %copy-done.26, f32[512]{0:T(512)S(1)} %get-tuple-element.91), kind=kOutput, calls=%fused_computation.16 | convolution fusion | flops 5911871488 | bytes 21506048 | tf_op jit(solution)/shard_map/td,cdf->ctf/dot_general | solution.py:509
  172.2 7.1 fusion.32
  180.4 8.5 %bitcast_convert_fusion = bf16[512,2048]{1,0:T(8,128)(2,1)} fusion(bf16[2,2048,1408]{2,1,0:T(8,128)(2,1)S(1)} %bitcast.120, bf16[1,512,1408]{2,1,0:T(8,128)(2,1)} %get-tuple-element.85, bf16[1,512,1408]{2,1,0:T(8,128)(2,1)S(1)} %get-tuple-element.84), kind=kOutput, calls=%fused_computation.31 | convolution fusion | flops 5908070400 | bytes 16515072 | tf_op jit(solution)/shard_map/ctf,cdf->td/dot_general | solution.py:509
  189.0 85.3 %all-reduce.10.cloned.1.call-done = bf16[512,2048]{1,0:T(8,128)(2,1)} async-done(((bf16[512,2048]{1,0:T(8,128)(2,1)}), bf16[512,2048]{1,0:T(8,128)(2,1)}) %all-reduce.10.cloned.1.call-update) | async-done | bytes 2097168 | tf_op jit(solution)/shard_map/psum | solution.py:548
  274.3 4.8 fusion.11
  279.1 3.6 fusion.10
  287.7 9.4 %convolution_convert_fusion.3 = bf16[512,2048]{1,0:T(8,128)(2,1)} fusion(bf16[1408,2048]{1,0:T(8,128)(2,1)} %param.20, f32[2,512,1408]{2,1,0:T(8,128)} %convolution_bitcast_fusion), kind=kOutput, calls=%fused_computation.38 | convolution fusion | flops 2958163968 | bytes 13631488 | tf_op jit(solution)/shard_map/tf,fd->td/dot_general | solution.py:509
  299.3 33.3 %delta_backward.1 = (bf16[3,512,512]{2,1,0:T(8,128)(2,1)}, bf16[512,512]{1,0:T(8,128)(2,1)}, bf16[512,128]{1,0:T(8,128)(2,1)}, f32[3,4,512]{2,1,0:T(4,128)}, f32[8,128]{1,0:T(8,128)}) custom-call(bf16[3,512,512]{2,1,0:T(8,128)(2,1)} %slice.64.raw, bf16[3,16,512]{2,1,0:T(8,128)(2,1)} %copy-done.11, f32[3,4,512]{2,1,0:T(4,128)} %conv_w.3, f32[512,4]{1,0:T(8,128)} %copy-done.4, ...), custom_call_target="tpu_custom_call" | custom-call | tf_op jit(solution)/shard_map/delta_backward/pallas_call | solution.py:477
  332.7 7.6 %fusion.35 = f32[512,2048,1]{1,0,2:T(8,128)S(1)} fusion(bf16[4,2048,512]{2,1,0:T(8,128)(2,1)} %param.13, bf16[1,512,512]{2,1,0:T(8,128)(2,1)} %bitcast.123, bf16[3,512,512]{2,1,0:T(8,128)(2,1)} %get-tuple-element.40), kind=kOutput, calls=%fused_computation.65 | convolution fusion | flops 4296015872 | bytes 14680064 | tf_op jit(solution)/shard_map/cte,cde->td/dot_general | solution.py:509
  343.9 7.9 %convolution_convert_fusion = bf16[1408,2048]{1,0:T(8,128)(2,1)} fusion(bf16[1,512,2048]{2,1,0:T(8,128)(2,1)S(1)} %copy-done.23, f32[2,512,1408]{2,1,0:T(8,128)} %convolution_bitcast_fusion), kind=kOutput, calls=%fused_computation.7 | convolution fusion | flops 2959998976 | bytes 13631488 | tf_op jit(solution)/shard_map/tf,td->fd/dot_general | solution.py:509
  353.5 8.4 %convert_bitcast_fusion.1 = bf16[4,2048,512]{1,2,0:T(8,128)(2,1)} fusion(bf16[1,512,512]{2,1,0:T(8,128)(2,1)S(1)} %bitcast.124, bf16[3,512,512]{2,1,0:T(8,128)(2,1)} %get-tuple-element.40, bf16[1,512,2048]{2,1,0:T(8,128)(2,1)S(1)} %copy-done.16, f32[2048]{0:T(1024)S(1)} %copy-done.25, f32[512]{0:T(512)S(1)} %get-tuple-element.89), kind=kOutput, calls=%fused_computation.6 | convolution fusion | flops 4304404480 | bytes 12593152 | tf_op jit(solution)/shard_map/td,cte->cde/dot_general | solution.py:509
  362.0 11.5 %convert_bitcast_fusion = bf16[2,2048,1408]{1,2,0:T(8,128)(2,1)} fusion(bf16[1,512,1408]{2,1,0:T(8,128)(2,1)} %get-tuple-element.85, bf16[1,512,1408]{2,1,0:T(8,128)(2,1)} %copy-done.31, bf16[512,2048]{1,0:T(8,128)(2,1)} %all-reduce.8.cloned.1.call-done, bf16[1,512,2048]{2,1,0:T(8,128)(2,1)S(1)} %copy-done.16, f32[2048]{0:T(1024)S(1)} %copy-done.26, ...), kind=kOutput, calls=%fused_computation | convolution fusion | flops 5919080448 | bytes 18622464 | tf_op jit(solution)/shard_map/td,ctf->cdf/dot_general | solution.py:509
  374.2 11.3 %all-reduce.1 = (f32[128]{0:T(128)S(1)}, f32[]{:T(128)}) all-reduce(f32[128]{0:T(128)S(1)} %reduce_sum.76, f32[]{:T(128)} %bitcast.21), channel_id=1, replica_groups=mesh['dp'=4,'seq'=2,'head'=4] {'head'}, use_global_device_ids=true, to_apply=%region_14.0 | all-reduce | flops 129 | bytes 1032 | tf_op jit(solution)/shard_map/psum | solution.py:568
  388.0 108.9 %all-reduce.12.cloned.1.call-done = (bf16[512,2048]{1,0:T(8,128)(2,1)}, bf16[512,2048]{1,0:T(8,128)(2,1)}) async-done(((bf16[512,2048]{1,0:T(8,128)(2,1)}, bf16[512,2048]{1,0:T(8,128)(2,1)}), (bf16[512,2048]{1,0:T(8,128)(2,1)}, bf16[512,2048]{1,0:T(8,128)(2,1)})) %all-reduce.12.cloned.1.call-update) | async-done | bytes 4194320 | tf_op jit(solution)/shard_map/psum | solution.py:541
  496.8 3.3 fusion.12
  500.2 25.5 %all-reduce.13 = (f32[2048]{0:T(1024)}, f32[2048,4]{0,1:T(4,128)}, f32[3,4,512]{2,1,0:T(4,128)}, f32[128]{0:T(128)}, f32[2048]{0:T(1024)}, /*index=5*/f32[]{:T(128)}) all-reduce(f32[2048]{0:T(1024)S(1)} %get-tuple-element.72, f32[2048,4]{0,1:T(4,128)S(1)} %fusion.42, ...), channel_id=1, replica_groups=mesh['dp'=4,'seq'=2,'head'=4] {'dp','seq'}, use_global_device_ids=true, to_apply=%region_9.0 | all-reduce | flops 18561 | bytes 148488 | tf_op jit(solution)/shard_map/psum | solution.py:569
  526.3 6.7 fusion.25
  533.0 25.1 %reduce-scatter.11.cloned.1.call-done = bf16[1408,256]{1,0:T(8,128)(2,1)} async-done(((bf16[1408,2048]{1,0:T(8,128)(2,1)}), bf16[1408,256]{1,0:T(8,128)(2,1)}) %reduce-scatter.11.cloned.1.call-update) | async-done | bytes 720912 | tf_op jit(solution)/shard_map/reduce_scatter | solution.py:573
  560.3 72.3 %reduce-scatter.5.cloned.1.call-done = bf16[4,256,512]{1,2,0:T(8,128)(2,1)} async-done(((bf16[4,2048,512]{1,2,0:T(8,128)(2,1)}), bf16[4,256,512]{1,2,0:T(8,128)(2,1)}) %reduce-scatter.5.cloned.1.call-update) | async-done | bytes 1048592 | tf_op jit(solution)/shard_map/reduce_scatter | solution.py:575
  635.4 87.6 %reduce-scatter.9.cloned.1.call-done = bf16[2,256,1408]{1,2,0:T(8,128)(2,1)} async-done(((bf16[2,2048,1408]{1,2,0:T(8,128)(2,1)}), bf16[2,256,1408]{1,2,0:T(8,128)(2,1)}) %reduce-scatter.9.cloned.1.call-update) | async-done | bytes 1441808 | tf_op jit(solution)/shard_map/reduce_scatter | solution.py:572
  (110 shorter events, 40.2 us)
Async XLA Ops:
  7.2 55.1 %copy-start = (bf16[512,2048]{1,0:T(8,128)(2,1)S(1)}, bf16[512,2048]{1,0:T(8,128)(2,1)}, u32[]{:S(2)}) copy-start(bf16[512,2048]{1,0:T(8,128)(2,1)} %param.17) | copy-start | bytes 6291460
  7.2 150.0 %all-reduce.8.cloned.1.call-start = ((), (), s32[]{:S(2)}) async-start(), calls=%async_computation.4 | async-start | bytes 4194304 | tf_op jit(solution)/shard_map/psum | solution.py:533
  20.5 44.3 %copy-start.4 = (f32[512,4]{1,0:T(8,128)}, f32[512,4]{1,0:T(8,128)S(1)}, u32[]{:S(2)}) copy-start(f32[512,4]{1,0:T(8,128)S(1)} %fusion.38.beta) | copy-start | bytes 24580
  64.9 95.5 %copy-start.26 = (f32[2048]{0:T(1024)S(1)}, f32[2048]{0:T(1024)}, u32[]{:S(2)}) copy-start(f32[2048]{0:T(1024)} %param.18) | copy-start | bytes 24580
  64.9 209.4 %all-reduce.10.cloned.1.call-start = ((), (), s32[]{:S(2)}) async-start(), calls=%async_computation.5 | async-start | bytes 4194304 | tf_op jit(solution)/shard_map/psum | solution.py:548
  157.2 3.5 copy-start.17
  157.2 15.0 %slice-start.3 = ((s8[5767168]{0:T(1024)(128)(4,1)}), s8[4194304]{0:T(1024)(128)(4,1)S(1)}, s32[]{:S(2)}) async-start(s8[5767168]{0:T(1024)(128)(4,1)} %bitcast.121), calls=%async_computation.14 | async-start | bytes 8388608
  160.7 11.5 %copy-start.22 = (bf16[1,512,2048]{2,1,0:T(8,128)(2,1)S(1)}, bf16[1,512,2048]{2,1,0:T(8,128)(2,1)}, u32[]{:S(2)}) copy-start(bf16[1,512,2048]{2,1,0:T(8,128)(2,1)} %param.21) | copy-start | bytes 6291460
  160.7 11.5 %slice-start.4 = ((s8[5767168]{0:T(1024)(128)(4,1)}), s8[1572864]{0:T(1024)(128)(4,1)S(1)}, s32[]{:S(2)}) async-start(s8[5767168]{0:T(1024)(128)(4,1)} %bitcast.121), calls=%async_computation.15 | async-start | bytes 3145728
  160.7 19.7 %slice-start = ((s8[11534336]{0:T(1024)(128)(4,1)}), s8[4194304]{0:T(1024)(128)(4,1)S(1)}, s32[]{:S(2)}) async-start(s8[11534336]{0:T(1024)(128)(4,1)} %bitcast.119), calls=%async_computation.11 | async-start | bytes 8388608
  160.7 19.7 %slice-start.1 = ((s8[11534336]{0:T(1024)(128)(4,1)}), s8[4194304]{0:T(1024)(128)(4,1)S(1)}, s32[]{:S(2)}) async-start(s8[11534336]{0:T(1024)(128)(4,1)} %bitcast.119), calls=%async_computation.12 | async-start | bytes 8388608
  172.2 8.2 %slice-start.2 = ((s8[11534336]{0:T(1024)(128)(4,1)}), s8[3145728]{0:T(1024)(128)(4,1)S(1)}, s32[]{:S(2)}) async-start(s8[11534336]{0:T(1024)(128)(4,1)} %bitcast.119), calls=%async_computation.13 | async-start | bytes 6291456
  189.0 197.2 %reduce-scatter.7.cloned.1.call-start = ((), (), s32[]{:S(2)}) async-start(), calls=%async_computation.7 | async-start | bytes 2359296 | tf_op jit(solution)/shard_map/reduce_scatter | solution.py:574
  274.3 4.8 copy-start.15
  274.3 4.8 copy-start.18
  274.3 4.8 copy-start.21
  287.4 209.4 %all-reduce.12.cloned.1.call-start = ((), (), s32[]{:S(2)}) async-start(), calls=%async_computation.10 | async-start | bytes 8388608 | tf_op jit(solution)/shard_map/psum | solution.py:541
  287.7 9.4 %copy-start.20 = (f32[512,2048]{1,0:T(8,128)S(1)}, f32[512,2048]{1,0:T(8,128)}, u32[]{:S(2)}) copy-start(f32[512,2048]{1,0:T(8,128)} %copy-done.19) | copy-start | bytes 12582916
  332.7 7.7 %copy-start.24 = (bf16[512,128]{1,0:T(8,128)(2,1)S(1)}, bf16[512,128]{1,0:T(8,128)(2,1)}, u32[]{:S(2)}) copy-start(bf16[512,128]{1,0:T(8,128)(2,1)} %get-tuple-element.42) | copy-start | bytes 393220
  342.4 215.6 %reduce-scatter.11.cloned.1.call-start = ((), (), s32[]{:S(2)}) async-start(), calls=%async_computation.9 | async-start | bytes 6488064 | tf_op jit(solution)/shard_map/reduce_scatter | solution.py:573
  351.8 280.8 %reduce-scatter.5.cloned.1.call-start = ((), (), s32[]{:S(2)}) async-start(), calls=%async_computation.6 | async-start | bytes 9437184 | tf_op jit(solution)/shard_map/reduce_scatter | solution.py:575
  361.9 361.1 %reduce-scatter.9.cloned.1.call-start = ((), (), s32[]{:S(2)}) async-start(), calls=%async_computation.8 | async-start | bytes 12976128 | tf_op jit(solution)/shard_map/reduce_scatter | solution.py:572
  386.2 114.0 %copy-start.27 = (f32[3,4,512]{2,1,0:T(4,128)S(1)}, f32[3,4,512]{2,1,0:T(4,128)}, u32[]{:S(2)}) copy-start(f32[3,4,512]{2,1,0:T(4,128)} %get-tuple-element.43) | copy-start | bytes 73732
  632.7 93.3 %copy-start.1 = (bf16[512,2048]{1,0:T(8,128)(2,1)S(1)}, bf16[512,2048]{1,0:T(8,128)(2,1)}, u32[]{:S(2)}) copy-start(bf16[512,2048]{1,0:T(8,128)(2,1)} %param.17) | copy-start | bytes 6291460
  (20 other events, 27.6 us)
Sparse Core Ops, SparseCore 0:
  65.0 92.1 all-reduce.7
  189.1 85.1 all-reduce.9
  287.6 40.3 reduce-scatter.6
  342.5 154.3 all-reduce.11
  500.1 57.8 reduce-scatter.10
  561.3 71.2 reduce-scatter.4
  636.2 86.8 reduce-scatter.8

commit v2 on v1

--- a/solution.py
+++ b/solution.py
@@ -10,6 +10,7 @@
 HD = 128
 SPAN = 64
 RIM = 16
+PIECE = 32
 
 
 MESH_ID = pl.DeviceIdType.MESH
@@ -85,13 +86,16 @@
     def _():
         pl.semaphore_signal(barrier, inc=1, device_id={axis: idx + 1}, device_id_type=MESH_ID)
 
-    @pl.when(idx > 0)
+    ends = (idx == 0) | (idx == count - 1)
+
+    @pl.when(ends)
     def _():
         pl.semaphore_wait(barrier, 1)
 
-    @pl.when(idx < count - 1)
-    def _():
-        pl.semaphore_wait(barrier, 1)
+    if count > 2:
+        @pl.when(jnp.logical_not(ends))
+        def _():
+            pl.semaphore_wait(barrier, 2)
 
 
 def send_to(src, dst, send_sem, recv_sem, axis, target):
@@ -283,6 +287,7 @@
         compiler_params=pltpu.CompilerParams(
             collective_id=0 if runs > 1 else None, has_side_effects=True, vmem_limit_bytes=48 << 20
         ),
+        cost_estimate=pl.CostEstimate(flops=0, transcendentals=0, bytes_accessed=count_rows * width * 400),
         name="delta_forward",
     )(raw, conv_w, beta, gate, gain.reshape(1, HD))
 
@@ -497,31 +502,261 @@
         compiler_params=pltpu.CompilerParams(
             collective_id=1 if runs > 1 else None, has_side_effects=True, vmem_limit_bytes=56 << 20
         ),
+        cost_estimate=pl.CostEstimate(flops=0, transcendentals=0, bytes_accessed=count_rows * width * 400),
         name="delta_backward",
     )(raw, rim, conv_w, beta, gate, gain.reshape(1, HD), q_s, k_s, w_s, u_s, t_s, p_s, f_s, s_s, o_s, d_gated)
 
 
+def plan_head_sum(size, subs, count):
+    tasks = {}
+    for g in range(count):
+        for s in range(subs):
+            for m in range(size):
+                for q in range(size - 1):
+                    tasks[(0, m, g, s, q)] = None
+                    tasks[(1, m, g, s, q + 1)] = None
+    done = {}
+
+    def ready(task):
+        way, m, g, s, q = task
+        j = size - 1 - m if way == 0 else m
+        back = q - 1 if way == 0 else q + 1
+        needs = []
+        if 0 <= back < size:
+            needs.append((way, m, g, s, back))
+        if j == q:
+            other = q + 1 if way == 0 else q - 1
+            if 0 <= other < size:
+                needs.append((1 - way, q if way == 0 else size - 1 - q, g, s, other))
+        times = [done.get(n) for n in needs]
+        if any(t is None for t in times):
+            return None
+        return max([0.0] + times)
+
+    free = {}
+    order = {p: [] for p in range(size)}
+    pending = set(tasks)
+    while pending:
+        best = None
+        for task in pending:
+            at = ready(task)
+            if at is None:
+                continue
+            link = (task[0], task[4])
+            start = max(at, free.get(link, 0.0))
+            key = (start, task[1], task[2], task[3], task[0], task[4])
+            if best is None or key < best[0]:
+                best = (key, task)
+        (start, *_), task = best
+        pending.remove(task)
+        free[(task[0], task[4])] = start + 1.0
+        done[task] = start + 1.0 + 0.5
+        order[task[4]].append(task[:4])
+    return order
+
+
+def head_sum_body(size, subs, parts, arrive, outs, finish, send_sems, recv_sems):
+    count = len(parts)
+    idx = lax.axis_index("head")
+    rows = parts[0].shape[0] // size
+    sub = rows // subs
+    orders = plan_head_sum(size, subs, count)
+    meet(idx, size, "head")
+
+    def at(j, s):
+        return pl.ds(j * rows + s * sub, sub)
+
+    def device(p):
+        waited, finals = set(), set()
+
+        def copy(way, m, g, s, to=None):
+            j = size - 1 - m if way == 0 else m
+            sender = p if to is not None else (p - 1 if way == 0 else p + 1)
+            summing = sender < j if way == 0 else sender > j
+            upstream = sender > 0 if way == 0 else sender < size - 1
+            dst = arrive[g][way] if summing else outs[g]
+            src = (arrive[g][way] if upstream else parts[g]) if summing else outs[g]
+            if to is None:
+                src = dst
+            n = ((g * subs + s) * 2 + way) * size + m
+            return pltpu.make_async_remote_copy(
+                src_ref=src.at[at(j, s), :],
+                dst_ref=dst.at[at(j, s), :],
+                send_sem=send_sems.at[n],
+                recv_sem=recv_sems.at[n],
+                device_id={"head": (p + 1 if way == 0 else p - 1) if to is not None else sender},
+                device_id_type=MESH_ID,
+            )
+
+        def has_upstream(way):
+            return p > 0 if way == 0 else p < size - 1
+
+        def need(way, m, g, s):
+            if has_upstream(way) and (way, m, g, s) not in waited:
+                copy(way, m, g, s).wait_recv()
+                waited.add((way, m, g, s))
+
+        for way, m, g, s in orders[p]:
+            j = size - 1 - m if way == 0 else m
+            if j == p:
+                if (g, s) not in finals:
+                    finals.add((g, s))
+                    need(0, size - 1 - p, g, s)
+                    need(1, p, g, s)
+                    sides = [arrive[g][w] for w in range(2) if has_upstream(w)]
+                    finish(g, p, s, sides)
+            else:
+                need(way, m, g, s)
+                summing = p < j if way == 0 else p > j
+                if summing and has_upstream(way):
+                    box = arrive[g][way]
+
+                    def add(i, carry, box=box, g=g, j=j, s=s):
+                        r = pl.ds(pl.multiple_of(j * rows + s * sub + i * 16, 16), 16)
+                        box[r, :] = (box[r, :].astype(F32) + parts[g][r, :].astype(F32)).astype(BF)
+                        return carry
+
+                    lax.fori_loop(0, sub // 16, add, 0)
+            copy(way, m, g, s, to=True).start()
+        for g in range(count):
+            for s in range(subs):
+                for way in range(2):
+                    for m in range(size):
+                        need(way, m, g, s)
+        for way, m, g, s in orders[p]:
+            copy(way, m, g, s, to=True).wait_send()
+
+    for p in range(size):
+        pl.when(idx == p)(functools.partial(device, p))
+
+
+def own_rows(p, s, i, rows, sub):
+    start = s * sub + i * 16
+    return (
+        pl.ds(pl.multiple_of(p * rows + start, 16), 16),
+        pl.ds(pl.multiple_of(start, 16), 16),
+    )
+
+
+def total_rows(part, sides, r):
+    total = part[r, :].astype(F32)
+    for side in sides:
+        total = total + side[r, :].astype(F32)
+    return total
+
+
+def norm_back_rows(x, gain, d):
+    r = lax.rsqrt(jnp.mean(x * x, axis=1, keepdims=True) + 1e-06)
+    e = d * gain
+    unit = x * r
+    gain_part = d * unit
+    return r * (e - unit * jnp.mean(e * unit, axis=1, keepdims=True)), gain_part
+
+
+def mixer_sum_kernel(size, subs, part, tokens, gain, hidden, normed, right, left, send_sems, recv_sems):
+    rows = part.shape[0] // size
+    sub = rows // subs
+
+    def finish(g, p, s, sides):
+        def step(i, carry):
+            r, own = own_rows(p, s, i, rows, sub)
+            x = tokens[r, :].astype(F32) + total_rows(part, sides, r)
+            hidden[own, :] = x
+            scale = lax.rsqrt(jnp.mean(x * x, axis=1, keepdims=True) + 1e-06)
+            normed[r, :] = (x * scale * gain[...]).astype(BF)
+            return carry
+
+        lax.fori_loop(0, sub // 16, step, 0)
+
+    head_sum_body(size, subs, [part], [(right, left)], [normed], finish, send_sems, recv_sems)
+
+
+def mlp_back_kernel(size, subs, part, hidden, cot, gain, d_hidden, gain_sum, d_attn, right, left, send_sems, recv_sems):
+    rows = part.shape[0] // size
+    sub = rows // subs
+    gain_sum[...] = jnp.zeros_like(gain_sum)
+
+    def finish(g, p, s, sides):
+        def step(i, carry):
+            r, own = own_rows(p, s, i, rows, sub)
+            back, gain_part = norm_back_rows(hidden[own, :], gain[...], total_rows(part, sides, r))
+            x = cot[r, :].astype(F32) + back
+            d_hidden[own, :] = x
+            d_attn[r, :] = x.astype(BF)
+            gain_sum[...] += jnp.sum(gain_part.reshape(2, 8, -1), axis=0)
+            return carry
+
+        lax.fori_loop(0, sub // 16, step, 0)
+
+    head_sum_body(size, subs, [part], [(right, left)], [d_attn], finish, send_sems, recv_sems)
+
+
+def last_sum_kernel(
+    size, subs, part, mlp_part, tokens, hidden, d_hidden, gain, gain_sum, d_tokens, result,
+    right, left, right2, left2, send_sems, recv_sems,
+):
+    rows = part.shape[0] // size
+    sub = rows // subs
+    gain_sum[...] = jnp.zeros_like(gain_sum)
+
+    def finish(g, p, s, sides):
+        def step(i, carry):
+            r, own = own_rows(p, s, i, rows, sub)
+            if g == 0:
+                back, gain_part = norm_back_rows(tokens[r, :].astype(F32), gain[...], total_rows(part, sides, r))
+                d_tokens[r, :] = (d_hidden[own, :] + back).astype(BF)
+                gain_sum[...] += jnp.sum(gain_part.reshape(2, 8, -1), axis=0)
+            else:
+                result[r, :] = (hidden[own, :] + total_rows(mlp_part, sides, r)).astype(BF)
+            return carry
+
+        lax.fori_loop(0, sub // 16, step, 0)
+
+    head_sum_body(
+        size, subs, [part, mlp_part], [(right, left), (right2, left2)], [d_tokens, result], finish, send_sems, recv_sems
+    )
+
+
+def head_sum_call(kernel, name, collective_id, size, sums, outs, *args):
+    count_rows, width = args[0].shape
+    subs = count_rows // size // PIECE
+    vmem = pl.BlockSpec(memory_space=pltpu.VMEM)
+    sems = pltpu.SemaphoreType.DMA((sums * subs * 2 * size,))
+    return pl.pallas_call(
+        functools.partial(kernel, size, subs),
+        out_shape=outs,
+        in_specs=[vmem] * len(args),
+        out_specs=[vmem] * len(outs),
+        scratch_shapes=[pltpu.VMEM((count_rows, width), BF)] * (2 * sums) + [sems, sems],
+        compiler_params=pltpu.CompilerParams(
+            collective_id=collective_id, has_side_effects=True, vmem_limit_bytes=56 << 20
+        ),
+        cost_estimate=pl.CostEstimate(flops=0, transcendentals=0, bytes_accessed=sums * count_rows * width * 64),
+        name=name,
+    )(*args)
+
+
 def inverse_rms(values):
     return lax.rsqrt(jnp.mean(values * values, axis=-1, keepdims=True) + 1e-06)
 
 
 def dot32(spec, a, b):
     return jnp.einsum(spec, a, b, preferred_element_type=F32)
-
-
-def norm_back(values, gain, d_values):
-    r = inverse_rms(values)
-    e = d_values * gain
-    grad_gain = jnp.sum(d_values * (values * r), axis=0)
-    return r * (e - values * (r * r) * jnp.mean(e * values, axis=-1, keepdims=True)), grad_gain
 
 
 def per_device(
     tokens, attn_gain, w_qkvg, w_beta, conv_w, out_gain, w_o, mlp_gain, w_gateup, w_down, cotangent
 ):
     runs = lax.axis_size("seq")
+    size = lax.axis_size("head")
     everyone = ("dp", "seq")
-    tok_rows = tokens[0].astype(F32)
+    tokens = tokens[0]
+    cot = cotangent[0]
+    count_rows, width = tokens.shape
+    own = count_rows // size
+    sd = jax.ShapeDtypeStruct
+    whole, mine, gain_rows = sd((count_rows, width), BF), sd((own, width), F32), sd((8, width), F32)
+    tok_rows = tokens.astype(F32)
     heads = w_beta.shape[1]
     normed = (tok_rows * inverse_rms(tok_rows) * attn_gain).astype(BF)
     projected = dot32("td,cde->cte", normed, w_qkvg)
@@ -530,65 +765,82 @@
     beta = jax.nn.sigmoid(dot32("td,dh->th", normed, w_beta))
     gated, *saved = delta_forward(raw, conv_w, beta, gate, out_gain, runs)
     norm_part = saved.pop()[0, 0]
-    attn = lax.psum(dot32("tc,cd->td", gated, w_o).astype(BF), "head").astype(F32)
-    hidden = tok_rows + attn
-    normed_mlp = (hidden * inverse_rms(hidden) * mlp_gain).astype(BF)
+    attn_part = dot32("tc,cd->td", gated, w_o).astype(BF)
+    hidden, normed_mlp = head_sum_call(
+        mixer_sum_kernel, "mixer_sum", 2, size, 1, [mine, whole], attn_part, tokens, mlp_gain.reshape(1, -1)
+    )
     gate_up = dot32("td,cdf->ctf", normed_mlp, w_gateup)
     gate_act, up_act = gate_up[0], gate_up[1]
     sig = jax.nn.sigmoid(gate_act)
     silu = gate_act * sig
     units = (silu * up_act).astype(BF)
-    mlp_out = lax.psum(dot32("tf,fd->td", units, w_down).astype(BF), "head").astype(F32)
-    result = (hidden + mlp_out).astype(BF)
-    cot = cotangent[0]
     d_hidden = dot32("td,fd->tf", cot, w_down)
     d_gate_up = jnp.stack(
         [d_hidden * up_act * (sig + silu * (1.0 - sig)), d_hidden * silu], axis=0
     ).astype(BF)
-    d_normed_mlp = lax.psum(dot32("ctf,cdf->td", d_gate_up, w_gateup).astype(BF), "head").astype(F32)
-    d_hidden_part, grad_mlp_gain = norm_back(hidden, mlp_gain, d_normed_mlp)
-    d_hidden_state = cot.astype(F32) + d_hidden_part
-    d_attn = d_hidden_state.astype(BF)
+    grad_mlp = jnp.concatenate(
+        [
+            dot32("td,ctf->cdf", normed_mlp, d_gate_up).astype(BF),
+            dot32("td,tf->df", cot, units).astype(BF)[None],
+        ],
+        axis=0,
+    )
+    mlp_back_part = dot32("ctf,cdf->td", d_gate_up, w_gateup).astype(BF)
+    grad_mlp, mlp_back_part = lax.optimization_barrier((grad_mlp, mlp_back_part))
+    sum_mlp = lax.psum_scatter(grad_mlp, everyone, scatter_dimension=1, tiled=True)
+    d_hidden_rows, mlp_gain_rows, d_attn = head_sum_call(
+        mlp_back_kernel, "mlp_back", 3, size, 1, [mine, gain_rows, whole],
+        mlp_back_part, hidden, cot, mlp_gain.reshape(1, -1),
+    )
+    mlp_part = dot32("tf,fd->td", units, w_down).astype(BF)
     d_gated = dot32("td,cd->tc", d_attn, w_o)
-    d_raw, d_gate, d_beta, grad_conv, grad_gain_rows = delta_backward(
+    d_raw, d_gate, d_beta, grad_conv, out_gain_rows = delta_backward(
         raw, conv_w, beta, gate, out_gain, saved, d_gated, runs
     )
     d_beta = d_beta[:, :heads]
     d_proj = jnp.concatenate([d_raw, d_gate[None]], axis=0)
-    d_normed = lax.psum(
-        (dot32("cte,cde->td", d_proj, w_qkvg) + dot32("th,dh->td", d_beta, w_beta)).astype(BF), "head"
-    ).astype(F32)
-    d_tok_part, grad_attn_gain = norm_back(tok_rows, attn_gain, d_normed)
-    d_tokens = (d_hidden_state + d_tok_part).astype(BF)
-    grad_down = dot32("tf,td->fd", units, cot).astype(BF)
-    grad_gateup = dot32("td,ctf->cdf", normed_mlp, d_gate_up).astype(BF)
-    grad_o = dot32("tc,td->cd", gated, d_attn).astype(BF)
-    grad_qkvg = dot32("td,cte->cde", normed, d_proj).astype(BF)
+    d_normed_part = (dot32("cte,cde->td", d_proj, w_qkvg) + dot32("th,dh->td", d_beta, w_beta)).astype(BF)
+    grad_mixer = jnp.concatenate(
+        [
+            dot32("td,cte->cde", normed, d_proj).astype(BF),
+            dot32("td,tc->dc", d_attn, gated).astype(BF)[None],
+        ],
+        axis=0,
+    )
     grad_beta = dot32("td,th->dh", normed, d_beta)
-    out_gain_head, norm_head = lax.psum((jnp.sum(grad_gain_rows, axis=0), norm_part), "head")
-    small = lax.psum(
-        (grad_attn_gain, grad_mlp_gain, out_gain_head, grad_conv, grad_beta, norm_head), everyone
-    )
-    sum_gateup = lax.psum_scatter(grad_gateup, everyone, scatter_dimension=1, tiled=True).astype(F32)
-    sum_down = lax.psum_scatter(grad_down, everyone, scatter_dimension=1, tiled=True).astype(F32)
-    sum_o = lax.psum_scatter(grad_o, everyone, scatter_dimension=1, tiled=True).astype(F32)
-    sum_qkvg = lax.psum_scatter(grad_qkvg, everyone, scatter_dimension=1, tiled=True).astype(F32)
-    state_mean = small[5] / (lax.axis_size("dp") * runs * heads * lax.axis_size("head"))
+    grad_mixer, d_normed_part, sum_mlp = lax.optimization_barrier((grad_mixer, d_normed_part, sum_mlp))
+    attn_gain_rows, d_tokens, result = head_sum_call(
+        last_sum_kernel, "last_sum", 4, size, 2, [gain_rows, whole, whole],
+        d_normed_part, mlp_part, tokens, hidden, d_hidden_rows, attn_gain.reshape(1, -1),
+    )
+    everywhere = lax.psum(
+        (
+            jnp.sum(attn_gain_rows, axis=0),
+            jnp.sum(mlp_gain_rows, axis=0),
+            jnp.sum(out_gain_rows, axis=0),
+            norm_part,
+        ),
+        ("dp", "seq", "head"),
+    )
+    small = lax.psum((grad_conv, grad_beta), everyone)
+    sum_mixer = lax.psum_scatter(grad_mixer, everyone, scatter_dimension=1, tiled=True)
+    sum_gateup, sum_down = sum_mlp[:2].astype(F32), sum_mlp[2].T.astype(F32)
+    sum_qkvg, sum_o = sum_mixer[:4].astype(F32), sum_mixer[4].T.astype(F32)
+    state_mean = everywhere[3] / (lax.axis_size("dp") * runs * heads * size)
     return (
         result[None],
         d_tokens[None],
+        everywhere[0],
+        sum_qkvg,
+        small[1],
         small[0],
-        sum_qkvg,
-        small[4],
-        small[3],
-        small[2],
+        everywhere[2],
         sum_o,
-        small[1],
+        everywhere[1],
         sum_gateup,
         sum_down,
         state_mean,
     )
-
 
 def solution(mesh):
     rows, halves_of = P("dp", "seq", None), P(None, None, "head")

time: 742 us -> 549 us (0.74)
  waiting for transfers between devices: 471 us -> 0.04 us
  Pallas kernels: 68.4 us -> 331 us
  blocking collectives: 36.8 us -> 62 us
    psum x3 -> x0, waiting for transfers between devices: 286 us -> none  [the longest x1 109 us: per_device(): lax.psum(dot32('tf,fd->td', units, w_down).astype(BF), 'head').astype(F32)]
    pallas_call x0 -> x3, Pallas kernels: none -> 260 us  [head_sum_call(): pl.pallas_call(functools.partial(kernel, size, subs), out_shape=outs, in_...]
    reduce_scatter x4 -> x2, waiting for transfers between devices: 185 us -> 0.01 us  [the longest x1 0.01 us: per_device(): lax.psum_scatter(grad_mlp, everyone, scatter_dimension=1, tiled=True)]
    psum x2, blocking collectives: 36.8 us -> 62 us  [the longest x1 38.6 us: per_device(): lax.psum((jnp.sum(attn_gain_rows, axis=0), jnp.sum(mlp_gain_rows, axis=0)...]
    concatenate x0 -> x2, other arithmetic: none -> 16 us  [the longest x1 8.95 us: per_device(): jnp.concatenate([dot32('td,cte->cde', normed, d_proj).astype(BF), dot32('...]
    unnamed x76 -> x60, local copies, waits for them, and re-layouts: 18.9 us -> 12.2 us
  transfers between devices with their start and end apart: 7 -> 2, of which waited for: 6 -> 0; matrix products, arithmetic and copies ran while one was open for 9% -> 10% of each run, Pallas kernels for 5% -> 42%
where the time goes in v2:
time: 549 us; the launch traced here: 539 us
  Pallas kernels  331 us (60%)
  matrix products  85.2 us (16%)
  blocking collectives  62 us (11%)
  other arithmetic  29.3 us (5%)
  between operations  16.5 us (3%)
  local copies, waits for them, and re-layouts  15.1 us (3%)
    pallas_call x3, Pallas kernels, head_sum_call(): pl.pallas_call(functools.partial(kernel, size, subs), out_shape=outs, in_...  260 us
    dot_general x15, matrix products, dot32(): return jnp.einsum(spec, a, b, preferred_element_type=F32)  85.2 us
    psum x1, blocking collectives, per_device(): lax.psum((jnp.sum(attn_gain_rows, axis=0), jnp.sum(mlp_gain_rows, axis=0)...  38.6 us
    pallas_call x1, Pallas kernels, delta_backward(): pl.pallas_call(functools.partial(delta_backward_kernel, heads, runs), out...  35.8 us
    pallas_call x1, Pallas kernels, delta_forward(): pl.pallas_call(functools.partial(delta_forward_kernel, heads, runs), out_...  35 us
    psum x1, blocking collectives, per_device(): small = lax.psum((grad_conv, grad_beta), everyone)  23.4 us
    unnamed x60, local copies, waits for them, and re-layouts  12.2 us
  transfers between devices with their start and end apart: 2, of which 0 were waited for; matrix products, arithmetic and copies ran while one was open for 10% of the time, Pallas kernels for 42%

profile of v2, /device:TPU:0, one launch (start us, length us, event | category | flops | bytes accessed | tf_op | source)
XLA Modules:
  0.0 539.2 jit_solution(11838008067077976452)
XLA Ops:
  9.5 7.8 %convolution_bitcast_fusion.1 = f32[4,512,512]{2,1,0:T(8,128)S(1)} fusion(bf16[4,2048,512]{2,1,0:T(8,128)(2,1)} %param.13, f32[2048]{0:T(1024)} %param.12, f32[512]{0:T(512)S(1)} %add_rsqrt_fusion, bf16[1,512,2048]{2,1,0:T(8,128)(2,1)} %param.11), kind=kOutput, calls=%fused_computation.33 | convolution fusion | flops 4299161600 | bytes 14690304 | tf_op jit(solution)/shard_map/td,cde->cte/dot_general | solution.py:744
  20.5 35.0 %delta_forward.1 = (bf16[512,512]{1,0:T(8,128)(2,1)S(1)}, bf16[8,256,128]{2,1,0:T(8,128)(2,1)S(1)}, bf16[8,256,128]{2,1,0:T(8,128)(2,1)S(1)}, bf16[8,256,128]{2,...) custom-call(bf16[3,512,512]{2,1,0:T(8,128)(2,1)} %slice.88.raw, ...), custom_call_target="tpu_custom_call" | custom-call | bytes 104857600 | tf_op jit(solution)/shard_map/delta_forward/pallas_call | solution.py:274
  55.6 2.8 convolution_convert_fusion.2.part
  58.5 68.5 %mixer_sum.1 = (f32[128,2048]{1,0:T(8,128)}, bf16[512,2048]{1,0:T(8,128)(2,1)}) custom-call(bf16[512,2048]{1,0:T(8,128)(2,1)} %convolution_convert_fusion.2.part, bf16[512,2048]{1,0:T(8,128)(2,1)} %bitcast.127, f32[1,2048]{1,0:T(1,128)} %bitcast.132), custom_call_target="tpu_custom_call" | custom-call | bytes 67108864 | tf_op jit(solution)/shard_map/mixer_sum/pallas_call | solution.py:725
  127.0 10.3 %convolution_bitcast_fusion = f32[2,512,1408]{2,1,0:T(8,128)S(1)} fusion(bf16[2,2048,1408]{2,1,0:T(8,128)(2,1)} %param.19, bf16[512,2048]{1,0:T(8,128)(2,1)} %get-tuple-element.53), kind=kOutput, calls=%fused_computation.8 | convolution fusion | flops 5905580032 | bytes 19398656 | tf_op jit(solution)/shard_map/td,cdf->ctf/dot_general | solution.py:744
  137.3 3.5 fusion
  140.8 6.7 %fusion.18 = (bf16[1,512,1408]{2,1,0:T(8,128)(2,1)S(1)}, bf16[1,512,1408]{2,1,0:T(8,128)(2,1)S(1)}) fusion(f32[2,512,1408]{2,1,0:T(8,128)S(1)} %convolution_bitcast_fusion, bf16[1408,2048]{1,0:T(8,128)(2,1)} %param.20, bf16[1,512,2048]{2,1,0:T(8,128)(2,1)S(1)} %copy-done.14), kind=kOutput, calls=%fused_computation.40 | convolution fusion | flops 2961440768 | bytes 16515072 | tf_op jit(solution)/shard_map/td,fd->tf/dot_general | solution.py:744
  148.6 10.1 %bitcast_convert_fusion.part = bf16[512,2048]{1,0:T(8,128)(2,1)} fusion(bf16[2,2048,1408]{2,1,0:T(8,128)(2,1)} %param.19, bf16[1,512,1408]{2,1,0:T(8,128)(2,1)S(1)} %get-tuple-element.103, bf16[1,512,1408]{2,1,0:T(8,128)(2,1)S(1)} %get-tuple-element.102), kind=kOutput, calls=%fused_computation.14 | convolution fusion | flops 5908070400 | bytes 16515072 | tf_op jit(solution)/shard_map/ctf,cdf->td/dot_general | solution.py:744
  158.8 8.3 %convert_bitcast_fusion = bf16[2,2048,1408]{1,2,0:T(8,128)(2,1)S(1)} fusion(bf16[512,2048]{1,0:T(8,128)(2,1)S(1)} %copy-done.23, bf16[1,512,1408]{2,1,0:T(8,128)(2,1)} %copy-done.27, bf16[1,512,1408]{2,1,0:T(8,128)(2,1)S(1)} %get-tuple-element.102), kind=kOutput, calls=%fused_computation.1 | convolution fusion | flops 5912788992 | bytes 16515072 | tf_op jit(solution)/shard_map/td,ctf->cdf/dot_general | solution.py:744
  167.1 7.1 %pad_maximum_fusion = bf16[3,2048,1408]{1,2,0:T(8,128)(2,1)} fusion(bf16[1,2048,1408]{1,2,0:T(8,128)(2,1)S(1)} %fusion, bf16[2,2048,1408]{1,2,0:T(8,128)(2,1)S(1)} %convert_bitcast_fusion), kind=kLoop, calls=%fused_computation | loop fusion | flops 8650752 | bytes 34603008 | tf_op jit(solution)/shard_map/concatenate | solution.py:781
  174.3 66.8 %mlp_back.1 = (f32[128,2048]{1,0:T(8,128)}, f32[8,2048]{1,0:T(8,128)}, bf16[512,2048]{1,0:T(8,128)(2,1)}) custom-call(bf16[512,2048]{1,0:T(8,128)(2,1)} %bitcast_convert_fusion.part, f32[128,2048]{1,0:T(8,128)} %get-tuple-element.55.hidden, bf16[512,2048]{1,0:T(8,128)(2,1)} %bitcast.129, f32[1,2048]{1,0:T(1,128)} %bitcast.133), custom_call_target="tpu_custom_call" | custom-call | bytes 67108864 | tf_op jit(solution)/shard_map/mlp_back/pallas_call | solution.py:725
  241.0 3.8 fusion.42.d_gated
  244.9 35.8 %delta_backward.1 = (bf16[3,512,512]{2,1,0:T(8,128)(2,1)}, bf16[512,512]{1,0:T(8,128)(2,1)}, bf16[512,128]{1,0:T(8,128)(2,1)}, f32[3,4,512]{2,1,0:T(4,128)}, f32[8,128]{1,0:T(8,128)}) custom-call(bf16[3,512,512]{2,1,0:T(8,128)(2,1)} %slice.88.raw, bf16[3,16,512]{2,1,0:T(8,128)(2,1)} %copy-done.10, f32[3,4,512]{2,1,0:T(4,128)} %conv_w.3, f32[512,4]{1,0:T(8,128)} %copy-done.3, ...), custom_call_target="tpu_custom_call" | custom-call | bytes 104857600 | tf_op jit(solution)/shard_map/delta_backward/pallas_call | solution.py:482
  283.4 7.2 %fusion.20 = f32[512,2048,1]{1,0,2:T(8,128)S(1)} fusion(bf16[4,2048,512]{2,1,0:T(8,128)(2,1)} %param.13, bf16[1,512,512]{2,1,0:T(8,128)(2,1)S(1)} %bitcast.135, bf16[3,512,512]{2,1,0:T(8,128)(2,1)S(1)} %copy-done.24), kind=kOutput, calls=%fused_computation.44 | convolution fusion | flops 4296015872 | bytes 14680064 | tf_op jit(solution)/shard_map/cte,cde->td/dot_general | solution.py:744
  292.7 7.1 %convert_bitcast_fusion.1 = bf16[4,2048,512]{1,2,0:T(8,128)(2,1)} fusion(bf16[1,512,512]{2,1,0:T(8,128)(2,1)S(1)} %bitcast.136, bf16[3,512,512]{2,1,0:T(8,128)(2,1)S(1)} %copy-done.24, f32[2048]{0:T(1024)S(1)} %copy-done.20, f32[512]{0:T(512)S(1)} %add_rsqrt_fusion, bf16[1,512,2048]{2,1,0:T(8,128)(2,1)S(1)} %copy-done.13), kind=kOutput, calls=%fused_computation.3 | convolution fusion | flops 4304404480 | bytes 12593152 | tf_op jit(solution)/shard_map/td,cte->cde/dot_general | solution.py:744
  299.8 8.9 %pad_maximum_fusion.1 = bf16[5,2048,512]{1,2,0:T(8,128)(2,1)} fusion(bf16[1,2048,512]{1,2,0:T(8,128)(2,1)} %fusion.11, bf16[4,2048,512]{1,2,0:T(8,128)(2,1)} %convert_bitcast_fusion.1), kind=kLoop, calls=%fused_computation.2 | loop fusion | flops 5242880 | bytes 20971520 | tf_op jit(solution)/shard_map/concatenate | solution.py:803
  311.9 23.4 %all-reduce.1 = (f32[2048,4]{0,1:T(4,128)}, f32[3,4,512]{2,1,0:T(4,128)}) all-reduce(f32[2048,4]{0,1:T(4,128)S(1)} %fusion.24, f32[3,4,512]{2,1,0:T(4,128)S(1)} %copy-done.18), channel_id=1, replica_groups=mesh['dp'=4,'seq'=2,'head'=4] {'dp','seq'}, use_global_device_ids=true, to_apply=%region_5.0 | all-reduce | flops 14336 | bytes 114688 | tf_op jit(solution)/shard_map/psum | solution.py:825
  335.3 9.8 %convolution_convert_fusion.3.mlp_part = bf16[512,2048]{1,0:T(8,128)(2,1)} fusion(bf16[1408,2048]{1,0:T(8,128)(2,1)} %param.20, f32[2,512,1408]{2,1,0:T(8,128)} %copy-done.26), kind=kOutput, calls=%fused_computation.18 | convolution fusion | flops 2958163968 | bytes 13631488 | tf_op jit(solution)/shard_map/tf,fd->td/dot_general | solution.py:744
  345.1 124.9 %last_sum.1 = (f32[8,2048]{1,0:T(8,128)}, bf16[512,2048]{1,0:T(8,128)(2,1)}, bf16[512,2048]{1,0:T(8,128)(2,1)}) custom-call(bf16[512,2048]{1,0:T(8,128)(2,1)} %fusion.4.part, bf16[512,2048]{1,0:T(8,128)(2,1)} %convolution_convert_fusion.3.mlp_part, bf16[512,2048]{1,0:T(8,128)(2,1)} %bitcast.128, f32[128,2048]{1,0:T(8,128)} %get-tuple-element.55.hidden, ...), custom_call_target="tpu_custom_call" | custom-call | bytes 134217728 | tf_op jit(solution)/shard_map/last_sum/pallas_call | solution.py:725
  470.9 3.2 slice_convert_fusion.1
  474.0 3.4 copy.36
  477.4 38.6 %all-reduce = (f32[2048]{0:T(1024)}, f32[128]{0:T(128)}, f32[2048]{0:T(1024)}, f32[]{:T(128)}) all-reduce(f32[2048]{0:T(1024)S(1)} %reduce_sum.37, f32[128]{0:T(128)S(1)} %reduce_sum.38, f32[2048]{0:T(1024)S(1)} %reduce_sum.39, f32[]{:T(128)} %bitcast.29), channel_id=1, replica_groups=mesh['dp'=4,'seq'=2,'head'=4] {'dp','seq','head'}, use_global_device_ids=true, to_apply=%region_3.0 | all-reduce | flops 4225 | bytes 33800 | tf_op jit(solution)/shard_map/psum | solution.py:816
  521.7 2.9 copy.35
  526.5 3.2 copy.43
  (78 shorter events, 23.6 us)
Async XLA Ops:
  7.2 48.4 %copy-start = (bf16[512,2048]{1,0:T(8,128)(2,1)S(1)}, bf16[512,2048]{1,0:T(8,128)(2,1)}, u32[]{:S(2)}) copy-start(bf16[512,2048]{1,0:T(8,128)(2,1)} %param.17) | copy-start | bytes 6291460
  7.2 301.6 %reduce-scatter.3.cloned.1.call-start = ((), (), s32[]{:S(2)}) async-start(), calls=%async_computation.2 | async-start | bytes 19464192 | tf_op jit(solution)/shard_map/reduce_scatter | solution.py:790
  17.2 2.4 copy-start.12
  17.2 2.4 copy-start.19
  17.3 2.4 copy-start.20
  20.5 37.9 %copy-start.3 = (f32[512,4]{1,0:T(8,128)}, f32[512,4]{1,0:T(8,128)S(1)}, u32[]{:S(2)}) copy-start(f32[512,4]{1,0:T(8,128)S(1)} %fusion.23.beta) | copy-start | bytes 24580
  55.5 2.9 copy-start.1
  55.5 2.9 copy-start.2
  55.6 2.9 copy-start.4
  55.6 2.9 copy-start.5
  55.6 2.9 copy-start.6
  55.6 2.9 copy-start.7
  55.6 2.9 copy-start.8
  55.6 2.9 copy-start.10
  127.0 10.3 %copy-start.14 = (bf16[1,512,2048]{2,1,0:T(8,128)(2,1)S(1)}, bf16[1,512,2048]{2,1,0:T(8,128)(2,1)}, u32[]{:S(2)}) copy-start(bf16[1,512,2048]{2,1,0:T(8,128)(2,1)} %param.21) | copy-start | bytes 6291460
  137.3 3.5 copy-start.26
  148.6 10.1 %copy-start.23 = (bf16[512,2048]{1,0:T(8,128)(2,1)S(1)}, bf16[512,2048]{1,0:T(8,128)(2,1)}, u32[]{:S(2)}) copy-start(bf16[512,2048]{1,0:T(8,128)(2,1)} %get-tuple-element.53) | copy-start | bytes 6291460
  174.2 344.8 %reduce-scatter.5.cloned.1.call-start = ((), (), s32[]{:S(2)}) async-start(), calls=%async_computation.3 | async-start | bytes 11796480 | tf_op jit(solution)/shard_map/reduce_scatter | solution.py:826
  244.9 35.9 %copy-start.22 = (bf16[512,2048]{1,0:T(8,128)(2,1)S(1)}, bf16[512,2048]{1,0:T(8,128)(2,1)}, u32[]{:S(2)}) copy-start(bf16[512,2048]{1,0:T(8,128)(2,1)} %get-tuple-element.56) | copy-start | bytes 6291460
  280.7 2.7 copy-start.24
  280.8 2.7 copy-start.25
  283.4 7.2 %copy-start.16 = (bf16[512,128]{1,0:T(8,128)(2,1)S(1)}, bf16[512,128]{1,0:T(8,128)(2,1)}, u32[]{:S(2)}) copy-start(bf16[512,128]{1,0:T(8,128)(2,1)} %get-tuple-element.59) | copy-start | bytes 393220
  308.8 3.1 copy-start.18
  524.6 5.1 copy-start.15
  (6 other events, 6.5 us)
Sparse Core Ops, SparseCore 0:
  174.3 121.1 reduce-scatter.2
  308.9 81.8 reduce-scatter.4
